TPU v7x, 32 devices: a whole 2x2x4 slice. The times are simulated.
32 devices in a mesh: seq: 2 (over y), batch: 4 (over z), head: 4 (over x, core).
Axes of the slice: x: 2, y: 2, z: 4, core: 2. Of those that a mesh axis runs over, the one named last changes fastest.
Arguments:
- tokens: bfloat16 [4, 1024, 768], P('batch', ('seq', 'head')), may hold values from -6 to 6
- seg_ids: int32 [4, 1024], P('batch'), may hold values from 0 to 11, never falling along the last dimension, each value on 1 to 512 neighbouring positions
- pattern: int32 [12, 16], P('head'), may hold values 0 or 1
- omega: float32 [64, 256], replicated, may hold values from -5 to 5
- norm1_gain: float32 [768], replicated, may hold values from 0.5 to 1.5
- norm1_bias: float32 [768], replicated, may hold values from -1.5 to 1.5
- w_qkv: bfloat16 [768, 3, 768], P(None, None, 'head'), may hold values from -0.21875 to 0.21875
- w_out: bfloat16 [768, 768], P('head'), may hold values from -0.875 to 0.875
- norm2_gain: float32 [768], replicated, may hold values from 0.5 to 1.5
- norm2_bias: float32 [768], replicated, may hold values from -1.5 to 1.5
- w_up: bfloat16 [768, 3072], P(None, 'head'), may hold values from -0.21875 to 0.21875
- w_down: bfloat16 [3072, 768], P('head'), may hold values from -0.109375 to 0.109375
- out_grad: bfloat16 [4, 1024, 768], P('batch', ('seq', 'head')), may hold values from -6 to 6
Outputs:
- mixed: bfloat16 [4, 1024, 768], P('batch', ('seq', 'head'))
- grad_tokens: float32 [4, 1024, 768], P('batch', ('seq', 'head'))
- grad_norm1_gain: float32 [768], P(('seq', 'batch', 'head'))
- grad_norm1_bias: float32 [768], P(('seq', 'batch', 'head'))
- grad_w_qkv: float32 [768, 3, 768], P(('seq', 'batch'), None, 'head')
- grad_w_out: float32 [768, 768], P('head', ('seq', 'batch'))
- grad_norm2_gain: float32 [768], P(('seq', 'batch', 'head'))
- grad_norm2_bias: float32 [768], P(('seq', 'batch', 'head'))
- grad_w_up: float32 [768, 3072], P(('seq', 'batch'), 'head')
- grad_w_down: float32 [3072, 768], P('head', ('seq', 'batch'))
Inputs may be any that keep to these rules, and one draw needn't show every extreme that they name: `seg_ids`: along a sequence the document numbers never fall; each document has 1 to 512 tokens and one has exactly that many.
All inputs are finite; a program needn't handle non-finite values. No bound on the sum of `pattern` on one device may be relied on, other than what follows from the above.
Results may differ from a plain program's by a relative error of at most 0.018.
Values may be sent and summed in bfloat16 or wider, within the bound.
A program may use at most 128 MiB of HBM per device.

v0:
```python
import math

import jax
import jax.numpy as jnp
from jax import lax
from jax.sharding import PartitionSpec as P

DH = 64
BLK = 64


def shifted(value, axis, steps):
    count = lax.axis_size(axis)
    first, last = (max(0, -steps), min(count, count - steps))
    return lax.ppermute(value, axis, [(source, source + steps) for source in range(first, last)])


def shortened(shard):
    return jax.tree.map(lambda a: a.astype(jnp.bfloat16) if a.dtype == jnp.float32 else a, shard)


def layer_norm(values, gain, bias):
    center = values - jnp.mean(values, axis=-1, keepdims=True)
    spread = jnp.mean(center * center, axis=-1, keepdims=True)
    return center * lax.rsqrt(spread + 1e-05) * gain + bias


def gelu_tanh(values):
    return jax.nn.gelu(values, approximate=True)


def feature_map(values, omega):
    depth = values.shape[-1]
    count = omega.shape[-1]
    scaled = values * depth ** (-0.25)
    projected = jnp.einsum("...td,dm->...tm", scaled, omega, precision=lax.Precision.HIGHEST)
    return jnp.exp(projected - 0.5 * jnp.sum(scaled * scaled, axis=-1, keepdims=True)) / math.sqrt(
        count
    )


def chain(feat_keys, values, segment):
    batch, heads, length, count = feat_keys.shape
    blocks = length // BLK
    seg_blocks = segment.reshape(batch, blocks, BLK)
    tail_ids = seg_blocks[:, :, -1]
    in_tail = (seg_blocks == tail_ids[:, :, None]).astype(jnp.float32)
    weighted = feat_keys.reshape(batch, heads, blocks, BLK, count) * in_tail[:, None, :, :, None]
    block_v = jnp.einsum(
        "shcjm,shcjd->shcmd",
        weighted,
        values.reshape(batch, heads, blocks, BLK, -1),
        precision=lax.Precision.HIGHEST,
    )
    block_z = jnp.sum(weighted, axis=3)
    positions = jnp.arange(blocks)
    linked = (
        (tail_ids[:, :, None] == tail_ids[:, None, :])
        & (positions[:, None] >= positions[None, :])[None]
    ).astype(jnp.float32)
    state_v = jnp.einsum("sbc,shcmd->shbmd", linked, block_v, precision=lax.Precision.HIGHEST)
    state_z = jnp.einsum("sbc,shcm->shbm", linked, block_z, precision=lax.Precision.HIGHEST)
    return (state_v, state_z, tail_ids)


def with_previous(current, first):
    earlier = jnp.concatenate([first[:, :, None], current[:, :, :-1]], axis=2)
    return jnp.concatenate([earlier, current], axis=3)


def attend(
    query,
    key_rows,
    value_rows,
    key_in,
    value_in,
    state_v_in,
    state_z_in,
    segment,
    seg_prev,
    tail_in,
    block_pattern,
    omega,
):
    batch, heads, length, depth = query.shape
    blocks = length // BLK
    feat_query = feature_map(query, omega)
    feat_keys = feature_map(key_rows, omega)
    feat_in = feature_map(key_in, omega)
    state_v, state_z, tail_ids = chain(feat_keys, value_rows, segment)
    carried = (tail_in[:, 1][:, None] == tail_ids).astype(jnp.float32)
    state_v = state_v + carried[:, None, :, None, None] * state_v_in[:, 1][:, :, None]
    state_z = state_z + carried[:, None, :, None] * state_z_in[:, 1][:, :, None]
    far_v = jnp.concatenate(
        [state_v_in[:, 0][:, :, None], state_v_in[:, 1][:, :, None], state_v[:, :, : blocks - 2]],
        axis=2,
    )
    far_z = jnp.concatenate(
        [state_z_in[:, 0][:, :, None], state_z_in[:, 1][:, :, None], state_z[:, :, : blocks - 2]],
        axis=2,
    )
    far_tail = jnp.concatenate([tail_in, tail_ids[:, : blocks - 2]], axis=1)
    seg_blocks = segment.reshape(batch, blocks, BLK)
    far_mask = (seg_blocks == far_tail[:, :, None]).astype(jnp.float32)
    query_feat_blocks = feat_query.reshape(batch, heads, blocks, BLK, -1)
    query_far = query_feat_blocks * far_mask[:, None, :, :, None]
    numer = jnp.einsum("shbim,shbmd->shbid", query_far, far_v, precision=lax.Precision.HIGHEST)
    denom = jnp.einsum("shbim,shbm->shbi", query_far, far_z, precision=lax.Precision.HIGHEST)
    query_blocks = query.reshape(batch, heads, blocks, BLK, depth)
    key_window = with_previous(key_rows.reshape(batch, heads, blocks, BLK, depth), key_in)
    value_window = with_previous(value_rows.reshape(batch, heads, blocks, BLK, depth), value_in)
    feat_window = with_previous(feat_keys.reshape(batch, heads, blocks, BLK, -1), feat_in)
    seg_earlier = jnp.concatenate([seg_prev[:, None], seg_blocks[:, :-1]], axis=1)
    seg_window = jnp.concatenate([seg_earlier, seg_blocks], axis=2)
    scores = jnp.einsum(
        "shbid,shbjd->shbij", query_blocks, key_window, precision=lax.Precision.HIGHEST
    ) / math.sqrt(depth)
    lowrank = jnp.einsum(
        "shbim,shbjm->shbij", query_feat_blocks, feat_window, precision=lax.Precision.HIGHEST
    )
    row_pos = jnp.arange(BLK)[:, None]
    col_pos = jnp.arange(2 * BLK)[None, :]
    causal = (col_pos < BLK) | (col_pos - BLK <= row_pos)
    same_doc = seg_blocks[:, :, :, None] == seg_window[:, :, None, :]
    allowed = (same_doc & causal[None, None]).astype(jnp.float32)[:, None]
    exact = jnp.where(col_pos >= BLK, 1.0, block_pattern.astype(jnp.float32)[:, :, None, None])
    weights = allowed * (exact * jnp.exp(scores) + (1.0 - exact) * lowrank)
    numer = numer + jnp.einsum(
        "shbij,shbjd->shbid", weights, value_window, precision=lax.Precision.HIGHEST
    )
    denom = denom + jnp.sum(weights, axis=-1)
    return (numer / denom[..., None]).reshape(batch, heads, length, depth)


def tail_pieces(key_rows, value_rows, segment, omega):
    state_v, state_z, tail_ids = chain(feature_map(key_rows, omega), value_rows, segment)
    return (
        key_rows[:, :, -BLK:],
        value_rows[:, :, -BLK:],
        jnp.moveaxis(state_v[:, :, -2:], 2, 1),
        jnp.moveaxis(state_z[:, :, -2:], 2, 1),
    )


def per_device(
    tokens,
    seg_ids,
    pattern,
    omega,
    norm1_gain,
    norm1_bias,
    w_qkv,
    w_out,
    norm2_gain,
    norm2_bias,
    w_up,
    w_down,
    out_grad,
):
    seq_pos = lax.axis_index("seq")
    half = seg_ids.shape[1] // lax.axis_size("seq")
    blocks = half // BLK
    local_pattern = lax.dynamic_slice_in_dim(pattern, seq_pos * blocks, blocks, 1)
    seg_half = lax.dynamic_slice_in_dim(seg_ids, seq_pos * half, half, 1)
    has_prior = seq_pos > 0
    seg_before = lax.dynamic_slice_in_dim(seg_ids, jnp.maximum(seq_pos * half - BLK, 0), BLK, 1)
    seg_older = lax.dynamic_slice_in_dim(seg_ids, jnp.maximum(seq_pos * half - BLK - 1, 0), 1, 1)
    seg_prev = jnp.where(has_prior, seg_before, -1)
    tail_in = jnp.where(has_prior, jnp.concatenate([seg_older, seg_before[:, -1:]], axis=1), -1)
    inputs = tokens.astype(jnp.float32)
    normed_one, pull_one = jax.vjp(layer_norm, inputs, norm1_gain, norm1_bias)
    gathered_one = lax.all_gather(normed_one.astype(jnp.bfloat16), "head", axis=1, tiled=True)
    qkv = jnp.einsum(
        "std,dce->stce", gathered_one, w_qkv, preferred_element_type=jnp.float32
    ).astype(jnp.bfloat16)
    batch, length = (gathered_one.shape[0], gathered_one.shape[1])
    local_heads = w_qkv.shape[2] // DH

    def split_heads(part):
        return (
            part.reshape(batch, length, local_heads, DH).transpose(0, 2, 1, 3).astype(jnp.float32)
        )

    def join_heads(part):
        return part.transpose(0, 2, 1, 3).reshape(batch, length, local_heads * DH)

    query, key_rows, value_rows = (
        split_heads(qkv[:, :, 0]),
        split_heads(qkv[:, :, 1]),
        split_heads(qkv[:, :, 2]),
    )

    def tail_fn(keys_local, values_local):
        return tail_pieces(keys_local, values_local, seg_half, omega)

    sent, pull_tail = jax.vjp(tail_fn, key_rows, value_rows)
    key_in, value_in, state_v_in, state_z_in = (
        shifted(sent[0].astype(jnp.bfloat16), "seq", 1).astype(jnp.float32),
        shifted(sent[1].astype(jnp.bfloat16), "seq", 1).astype(jnp.float32),
        shifted(sent[2].astype(jnp.bfloat16), "seq", 1).astype(jnp.float32),
        shifted(sent[3].astype(jnp.bfloat16), "seq", 1).astype(jnp.float32),
    )

    def attn_fn(
        query_local, keys_local, values_local, key_prior, value_prior, state_v_prior, state_z_prior
    ):
        return attend(
            query_local,
            keys_local,
            values_local,
            key_prior,
            value_prior,
            state_v_prior,
            state_z_prior,
            seg_half,
            seg_prev,
            tail_in,
            local_pattern,
            omega,
        )

    attn_inputs = (query, key_rows, value_rows, key_in, value_in, state_v_in, state_z_in)
    attended = attn_fn(*attn_inputs)
    attended_rows = join_heads(attended).astype(jnp.bfloat16)
    branch_term = jnp.einsum(
        "ste,ed->std", attended_rows, w_out, preferred_element_type=jnp.float32
    )
    hidden_one = inputs + lax.psum_scatter(
        branch_term.astype(jnp.bfloat16), "head", scatter_dimension=1, tiled=True
    ).astype(jnp.float32)
    normed_two, pull_two = jax.vjp(layer_norm, hidden_one, norm2_gain, norm2_bias)
    normed_two_low = normed_two.astype(jnp.bfloat16)
    gathered_two = lax.all_gather(normed_two_low, "head", axis=1, tiled=True)
    upper = jnp.einsum("std,df->stf", gathered_two, w_up, preferred_element_type=jnp.float32)
    activated, pull_act = jax.vjp(gelu_tanh, upper)
    activated = activated.astype(jnp.bfloat16)
    down_term = jnp.einsum("stf,fd->std", activated, w_down, preferred_element_type=jnp.float32)
    mixed = (
        hidden_one
        + lax.psum_scatter(
            down_term.astype(jnp.bfloat16), "head", scatter_dimension=1, tiled=True
        ).astype(jnp.float32)
    ).astype(jnp.bfloat16)
    grad_rows = lax.all_gather(out_grad, "head", axis=1, tiled=True)
    grad_down = jnp.einsum("stf,std->fd", activated, grad_rows, preferred_element_type=jnp.float32)
    grad_act = jnp.einsum("std,fd->stf", grad_rows, w_down, preferred_element_type=jnp.float32)
    grad_upper = pull_act(grad_act)[0].astype(jnp.bfloat16)
    grad_up = jnp.einsum(
        "std,stf->df", gathered_two, grad_upper, preferred_element_type=jnp.float32
    )
    grad_normed_two = lax.psum_scatter(
        jnp.einsum("stf,df->std", grad_upper, w_up, preferred_element_type=jnp.float32).astype(
            jnp.bfloat16
        ),
        "head",
        scatter_dimension=1,
        tiled=True,
    ).astype(jnp.float32)
    grad_hidden_ln, grad_gain_two, grad_bias_two = pull_two(grad_normed_two)
    grad_hidden = out_grad.astype(jnp.float32) + grad_hidden_ln
    grad_branch = lax.all_gather(grad_hidden.astype(jnp.bfloat16), "head", axis=1, tiled=True)
    grad_out = jnp.einsum(
        "ste,std->ed", attended_rows, grad_branch, preferred_element_type=jnp.float32
    )
    grad_attended = jnp.einsum(
        "std,ed->ste", grad_branch, w_out, preferred_element_type=jnp.float32
    )
    grad_attended = grad_attended.reshape(batch, length, local_heads, DH).transpose(0, 2, 1, 3)
    attended_again, pull_attn = jax.vjp(attn_fn, *attn_inputs)
    grad_query, grad_key, grad_value, grad_key_in, grad_value_in, grad_state_v, grad_state_z = (
        pull_attn(grad_attended)
    )
    returned = (
        shifted(shortened(grad_key_in), "seq", -1).astype(grad_key_in.dtype),
        shifted(shortened(grad_value_in), "seq", -1).astype(grad_value_in.dtype),
        shifted(shortened(grad_state_v), "seq", -1).astype(grad_state_v.dtype),
        shifted(shortened(grad_state_z), "seq", -1).astype(grad_state_z.dtype),
    )
    grad_key_tail, grad_value_tail = pull_tail((returned[0], returned[1], returned[2], returned[3]))
    grad_key = grad_key + grad_key_tail
    grad_value = grad_value + grad_value_tail
    grad_qkv = jnp.stack(
        [join_heads(grad_query), join_heads(grad_key), join_heads(grad_value)], axis=2
    ).astype(jnp.bfloat16)
    grad_qkv_weight = jnp.einsum(
        "std,stce->dce", gathered_one, grad_qkv, preferred_element_type=jnp.float32
    )
    grad_normed_one = lax.psum_scatter(
        jnp.einsum("stce,dce->std", grad_qkv, w_qkv, preferred_element_type=jnp.float32).astype(
            jnp.bfloat16
        ),
        "head",
        scatter_dimension=1,
        tiled=True,
    ).astype(jnp.float32)
    grad_input_ln, grad_gain_one, grad_bias_one = pull_one(grad_normed_one)
    grad_tokens = grad_hidden + grad_input_ln
    norm_sums = lax.psum_scatter(
        jnp.stack([grad_gain_one, grad_bias_one, grad_gain_two, grad_bias_two]),
        ("seq", "batch", "head"),
        scatter_dimension=1,
        tiled=True,
    )
    summed_qkv, summed_out, summed_up, summed_down = (
        lax.psum_scatter(grad_qkv_weight, ("seq", "batch"), scatter_dimension=0, tiled=True),
        lax.psum_scatter(grad_out, ("seq", "batch"), scatter_dimension=1, tiled=True),
        lax.psum_scatter(grad_up, ("seq", "batch"), scatter_dimension=0, tiled=True),
        lax.psum_scatter(grad_down, ("seq", "batch"), scatter_dimension=1, tiled=True),
    )
    return (
        mixed,
        grad_tokens,
        norm_sums[0],
        norm_sums[1],
        summed_qkv,
        summed_out,
        norm_sums[2],
        norm_sums[3],
        summed_up,
        summed_down,
    )


def solution(mesh):
    placed = (
        P("batch", ("seq", "head"), None),
        P("batch", None),
        P("head", None),
        P(),
        P(),
        P(),
        P(None, None, "head"),
        P("head", None),
        P(),
        P(),
        P(None, "head"),
        P("head", None),
        P("batch", ("seq", "head"), None),
    )
    return jax.shard_map(
        per_device,
        mesh=mesh,
        in_specs=placed,
        out_specs=(
            P("batch", ("seq", "head"), None),
            P("batch", ("seq", "head"), None),
            P(("seq", "batch", "head")),
            P(("seq", "batch", "head")),
            P(("seq", "batch"), None, "head"),
            P("head", ("seq", "batch")),
            P(("seq", "batch", "head")),
            P(("seq", "batch", "head")),
            P(("seq", "batch"), "head"),
            P("head", ("seq", "batch")),
        ),
        check_vma=False,
    )
```

profile of v0, /device:TPU:0, one launch (start us, length us, event | category | flops | bytes accessed | tf_op | source)
XLA Modules:
  0.0 562.7 jit_solution(15865716589194140890)
XLA Ops:
  15.5 10.0 %all_gather.12 = bf16[1,512,768]{2,1,0:T(8,128)(2,1)S(1)} all-gather(bf16[1,128,768]{2,1,0:T(8,128)(2,1)S(1)} %fusion.130), channel_id=1, replica_groups=mesh['seq'=2,'batch'=4,'head'=4] {'head'}, dimensions={1}, use_global_device_ids=true | all-gather | bytes 983040 | tf_op jit(solution)/shard_map/all_gather | solution.py:172
  29.1 2.8 broadcast_multiply_fusion
  37.1 4.2 collective-permute-start
  48.9 3.4 broadcast_multiply_fusion.1
  66.3 3.5 fusion.226
  76.6 3.1 divide_convert_fusion
  82.7 2.4 fusion.57
  85.1 10.1 %all_gather.14 = bf16[1,512,768]{2,1,0:T(8,128)(2,1)} all-gather(bf16[1,128,768]{2,1,0:T(8,128)(2,1)} %param.25), channel_id=1, replica_groups=mesh['seq'=2,'batch'=4,'head'=4] {'head'}, dimensions={1}, use_global_device_ids=true | all-gather | bytes 983040 | tf_op jit(solution)/shard_map/all_gather | solution.py:244
  95.2 13.2 %reduce-scatter.12.cloned.1.call-done = bf16[1,128,768]{2,1,0:T(8,128)(2,1)} async-done(((bf16[1,512,768]{2,1,0:T(8,128)(2,1)}), bf16[1,128,768]{2,1,0:T(8,128)(2,1)}) %reduce-scatter.12.cloned.1.call-update) | async-done | bytes 196624 | tf_op jit(solution)/shard_map/reduce_scatter | solution.py:228
  112.2 8.2 %all_gather.13 = bf16[1,512,768]{2,1,0:T(8,128)(2,1)S(1)} all-gather(bf16[1,128,768]{2,1,0:T(8,128)(2,1)S(1)} %add_convert_fusion.4), channel_id=1, replica_groups=mesh['seq'=2,'batch'=4,'head'=4] {'head'}, dimensions={1}, use_global_device_ids=true | all-gather | bytes 983040 | tf_op jit(solution)/shard_map/all_gather | solution.py:233
  127.1 3.7 fusion.58
  131.3 19.6 %reduce-scatter.16.cloned.1.call-done = bf16[1,128,768]{2,1,0:T(8,128)(2,1)} async-done(((bf16[1,512,768]{2,1,0:T(8,128)(2,1)}), bf16[1,128,768]{2,1,0:T(8,128)(2,1)}) %reduce-scatter.16.cloned.1.call-update) | async-done | bytes 196624 | tf_op jit(solution)/shard_map/reduce_scatter | solution.py:251
  153.9 22.9 %reduce-scatter.14.cloned.1.call-done = bf16[1,128,768]{2,1,0:T(8,128)(2,1)} async-done(((bf16[1,512,768]{2,1,0:T(8,128)(2,1)}), bf16[1,128,768]{2,1,0:T(8,128)(2,1)}) %reduce-scatter.14.cloned.1.call-update) | async-done | bytes 196624 | tf_op jit(solution)/shard_map/reduce_scatter | solution.py:240
  179.6 8.4 %all_gather.15 = bf16[1,512,768]{2,1,0:T(8,128)(2,1)S(1)} all-gather(bf16[1,128,768]{2,1,0:T(8,128)(2,1)S(1)} %fusion.148), channel_id=1, replica_groups=mesh['seq'=2,'batch'=4,'head'=4] {'head'}, dimensions={1}, use_global_device_ids=true | all-gather | bytes 983040 | tf_op jit(solution)/shard_map/all_gather | solution.py:261
  192.9 3.1 multiply_multiply_fusion.2
  196.0 2.4 fusion.156
  199.8 3.1 fusion
  202.9 2.9 convolution_bitcast_fusion
  222.1 4.4 add_multiply_fusion
  237.4 4.0 fusion.10
  246.9 3.7 fusion.88
  250.6 3.8 fusion.75
  260.1 2.3 pad_bitcast_fusion
  267.5 2.4 fusion.87
  274.7 3.3 add_convert_fusion.1
  283.2 3.9 fusion.95
  291.2 20.6 %reduce-scatter.26.cloned.1.call-done = f32[96,192]{1,0:T(8,128)} async-done(((f32[768,192]{1,0:T(8,128)}), f32[96,192]{1,0:T(8,128)}) %reduce-scatter.26.cloned.1.call-update) | async-done | bytes 73744
  313.4 23.0 %reduce-scatter.18.cloned.1.call-done = bf16[1,128,768]{2,1,0:T(8,128)(2,1)} async-done(((bf16[1,512,768]{2,1,0:T(8,128)(2,1)}), bf16[1,128,768]{2,1,0:T(8,128)(2,1)}) %reduce-scatter.18.cloned.1.call-update) | async-done | bytes 196624 | tf_op jit(solution)/shard_map/reduce_scatter | solution.py:288
  338.9 40.4 %all-reduce.15 = f32[4,768]{1,0:T(4,128)S(1)} all-reduce(f32[4,768]{1,0:T(4,128)S(1)} %pad_maximum_fusion.4), channel_id=6, replica_groups=mesh['seq'=2,'batch'=4,'head'=4] {'seq','batch','head'}, use_global_device_ids=true, to_apply=%region_28.29.clone | all-reduce | flops 3072 | bytes 24576
  381.8 28.9 %reduce-scatter.22.cloned.1.call-done = f32[96,768]{1,0:T(8,128)} async-done(((f32[768,768]{1,0:T(8,128)}), f32[96,768]{1,0:T(8,128)}) %reduce-scatter.22.cloned.1.call-update) | async-done | bytes 294928 | tf_op jit(solution)/shard_map/reduce_scatter | solution.py:307
  410.7 72.5 %reduce-scatter.24.cloned.1.call-done = f32[768,96]{0,1:T(8,128)} async-done(((f32[768,768]{0,1:T(8,128)}), f32[768,96]{0,1:T(8,128)}) %reduce-scatter.24.cloned.1.call-update) | async-done | bytes 294928 | tf_op jit(solution)/shard_map/reduce_scatter | solution.py:308
  483.1 72.5 %reduce-scatter.20.cloned.1.call-done = f32[96,3,192]{2,0,1:T(8,128)} async-done(((f32[768,3,192]{2,0,1:T(8,128)}), f32[96,3,192]{2,0,1:T(8,128)}) %reduce-scatter.20.cloned.1.call-update) | async-done | bytes 221200 | tf_op jit(solution)/shard_map/reduce_scatter | solution.py:305
  (407 shorter events, 134.0 us)
Async XLA Ops:
  7.2 114.2 %copy-start = (bf16[768,768]{1,0:T(8,128)(2,1)S(1)}, bf16[768,768]{1,0:T(8,128)(2,1)}, u32[]{:S(2)}) copy-start(bf16[768,768]{1,0:T(8,128)(2,1)} %param.23) | copy-start | bytes 3538948
  7.2 101.2 %reduce-scatter.12.cloned.1.call-start = ((), (), s32[]{:S(2)}) async-start(), calls=%async_computation.8 | async-start | bytes 983040 | tf_op jit(solution)/shard_map/reduce_scatter | solution.py:228
  9.4 44.5 %copy-start.84 = (s32[8]{0:T(128)}, s32[8]{0:T(128)S(1)}, u32[]{:S(2)}) copy-start(s32[8]{0:T(128)S(1)} %slice_reduce_fusion) | copy-start | bytes 100
  29.1 16.8 %copy-start.66 = (f32[8,64]{1,0:T(8,128)}, f32[8,64]{1,0:T(8,128)S(1)}, u32[]{:S(2)}) copy-start(f32[8,64]{1,0:T(8,128)S(1)} %get-tuple-element.45) | copy-start | bytes 6148
  29.1 32.3 %copy-start.72 = (f32[8,64]{1,0:T(8,128)}, f32[8,64]{1,0:T(8,128)S(1)}, u32[]{:S(2)}) copy-start(f32[8,64]{1,0:T(8,128)S(1)} %get-tuple-element.44) | copy-start | bytes 6148
  37.1 35.7 %collective-permute-start = (bf16[1,2,3,256,64]{3,0,4,2,1:T(2,128)(2,1)}, bf16[1,2,3,256,64]{3,0,4,2,1:T(2,128)(2,1)}, u32[]{:S(2)}, u32[]{:S(2)}) collective-permute-start(bf16[1,2,3,256,64]{3,0,4,2,1:T(2,128)(2,1)} %bitcast.434), channel_id=1, source_target_pairs={{0,16},{1,17},{2,18},{3,19},{4,20},{5,21},{6,22},{7,23},{8,24},{9,... | collective-permute-start | bytes 589832 | tf_op jit(solution)/shard_map/ppermute | solution.py:15
  42.0 22.3 %collective-permute-start.1 = (bf16[1,3,64,64]{2,3,1,0:T(8,128)(2,1)}, bf16[1,3,64,64]{2,3,1,0:T(8,128)(2,1)S(1)}, u32[]{:S(2)}, u32[]{:S(2)}) collective-permute-start(bf16[1,3,64,64]{2,3,1,0:T(8,128)(2,1)} %slice.136), channel_id=1, source_target_pairs={{0,16},{1,17},{2,18},{3,19},{4,20},{5,21},{6,22},{7,23},{8,24},{9,... | collective-permute-start | bytes 73736 | tf_op jit(solution)/shard_map/ppermute | solution.py:15
  44.0 25.8 %collective-permute-start.2 = (bf16[1,3,64,64]{2,3,1,0:T(8,128)(2,1)}, bf16[1,3,64,64]{2,3,1,0:T(8,128)(2,1)}, u32[]{:S(2)}, u32[]{:S(2)}) collective-permute-start(bf16[1,3,64,64]{2,3,1,0:T(8,128)(2,1)} %slice.139), channel_id=1, source_target_pairs={{0,16},{1,17},{2,18},{3,19},{4,20},{5,21},{6,22},{7,23},{8,24},{9,... | collective-permute-start | bytes 73736 | tf_op jit(solution)/shard_map/ppermute | solution.py:15
  46.3 14.3 %collective-permute-start.3 = (bf16[1,2,3,256]{3,0,2,1:T(2,128)(2,1)S(1)}, bf16[1,2,3,256]{3,0,2,1:T(2,128)(2,1)S(1)}, u32[]{:S(2)}, u32[]{:S(2)}) collective-permute-start(bf16[1,2,3,256]{3,0,2,1:T(2,128)(2,1)S(1)} %bitcast.498), channel_id=1, source_target_pairs={{0,16},{1,17},{2,18},{3,19},{4,20},{5,21},{6,22},{7,23},{8,24},{9,... | collective-permute-start | bytes 9224 | tf_op jit(solution)/shard_map/ppermute | solution.py:15
  82.7 25.7 %copy-start.6 = (bf16[1,128,768]{2,1,0:T(8,128)(2,1)S(1)}, bf16[1,128,768]{2,1,0:T(8,128)(2,1)}, u32[]{:S(2)}) copy-start(bf16[1,128,768]{2,1,0:T(8,128)(2,1)} %param.13) | copy-start | bytes 589828
  85.1 65.8 %reduce-scatter.16.cloned.1.call-start = ((), (), s32[]{:S(2)}) async-start(), calls=%async_computation.10 | async-start | bytes 983040 | tf_op jit(solution)/shard_map/reduce_scatter | solution.py:251
  127.1 49.7 %reduce-scatter.14.cloned.1.call-start = ((), (), s32[]{:S(2)}) async-start(), calls=%async_computation.9 | async-start | bytes 983040 | tf_op jit(solution)/shard_map/reduce_scatter | solution.py:240
  130.9 20.0 %copy-start.26 = (bf16[1,128,768]{2,1,0:T(8,128)(2,1)S(1)}, bf16[1,128,768]{2,1,0:T(8,128)(2,1)}, u32[]{:S(2)}) copy-start(bf16[1,128,768]{2,1,0:T(8,128)(2,1)} %reduce-scatter.12.cloned.1.call-done) | copy-start | bytes 589828
  130.9 48.6 %copy-start.50 = (bf16[1,128,768]{2,1,0:T(8,128)(2,1)S(1)}, bf16[1,128,768]{2,1,0:T(8,128)(2,1)}, u32[]{:S(2)}) copy-start(bf16[1,128,768]{2,1,0:T(8,128)(2,1)} %param.25) | copy-start | bytes 589828
  130.9 180.9 %reduce-scatter.26.cloned.1.call-start = ((), (), s32[]{:S(2)}) async-start(), calls=%async_computation.15 | async-start | bytes 884736
  192.8 16.8 %copy-start.75 = (f32[3,8,64]{2,1,0:T(8,128)}, f32[3,8,64]{2,1,0:T(8,128)S(1)}, u32[]{:S(2)}) copy-start(f32[3,8,64]{2,1,0:T(8,128)S(1)} %neg.28) | copy-start | bytes 18436
  236.1 38.5 %collective-permute-start.4 = (bf16[1,3,64,64]{2,3,1,0:T(8,128)(2,1)}, bf16[1,3,64,64]{2,3,1,0:T(8,128)(2,1)S(1)}, u32[]{:S(2)}, u32[]{:S(2)}) collective-permute-start(bf16[1,3,64,64]{2,3,1,0:T(8,128)(2,1)} %fusion.165), channel_id=1, source_target_pairs={{16,0},{17,1},{18,2},{19,3},{20,4},{21,5},{22,6},{23,7},{24,8},{25... | collective-permute-start | bytes 73736 | tf_op jit(solution)/shard_map/ppermute | solution.py:15
  242.8 16.5 %collective-permute-start.5 = (bf16[1,2,3,256]{3,0,2,1:T(2,128)(2,1)S(1)}, bf16[1,2,3,256]{3,0,2,1:T(2,128)(2,1)S(1)}, u32[]{:S(2)}, u32[]{:S(2)}) collective-permute-start(bf16[1,2,3,256]{3,0,2,1:T(2,128)(2,1)S(1)} %add_convert_fusion.5), channel_id=1, source_target_pairs={{16,0},{17,1},{18,2},{19,3},{20,4},{21,5},{22,6},{23,7},{24,8},{25... | collective-permute-start | bytes 9224 | tf_op jit(solution)/shard_map/ppermute | solution.py:15
  245.5 14.6 %collective-permute-start.6 = (bf16[1,2,3,256,64]{3,0,4,2,1:T(2,128)(2,1)}, bf16[1,2,3,256,64]{3,0,4,2,1:T(2,128)(2,1)}, u32[]{:S(2)}, u32[]{:S(2)}) collective-permute-start(bf16[1,2,3,256,64]{3,0,4,2,1:T(2,128)(2,1)} %add_convert_fusion.2), channel_id=1, source_target_pairs={{16,0},{17,1},{18,2},{19,3},{20,4},{21,5},{22,6},{23,7},{24,8},{25... | collective-permute-start | bytes 589832 | tf_op jit(solution)/shard_map/ppermute | solution.py:15
  246.8 89.6 %reduce-scatter.18.cloned.1.call-start = ((), (), s32[]{:S(2)}) async-start(), calls=%async_computation.11 | async-start | bytes 983040 | tf_op jit(solution)/shard_map/reduce_scatter | solution.py:288
  257.9 15.5 %collective-permute-start.7 = (bf16[1,3,64,64]{2,3,1,0:T(8,128)(2,1)S(1)}, bf16[1,3,64,64]{2,3,1,0:T(8,128)(2,1)S(1)}, u32[]{:S(2)}, u32[]{:S(2)}) collective-permute-start(bf16[1,3,64,64]{2,3,1,0:T(8,128)(2,1)S(1)} %copy-done.79), channel_id=1, source_target_pairs={{16,0},{17,1},{18,2},{19,3},{20,4},{21,5},{22,6},{23,7},{24,8},{25... | collective-permute-start | bytes 73736 | tf_op jit(solution)/shard_map/ppermute | solution.py:15
  279.8 130.8 %reduce-scatter.22.cloned.1.call-start = ((), (), s32[]{:S(2)}) async-start(), calls=%async_computation.13 | async-start | bytes 2654208 | tf_op jit(solution)/shard_map/reduce_scatter | solution.py:307
  282.1 201.0 %reduce-scatter.24.cloned.1.call-start = ((), (), s32[]{:S(2)}) async-start(), calls=%async_computation.14 | async-start | bytes 2654208 | tf_op jit(solution)/shard_map/reduce_scatter | solution.py:308
  287.1 268.5 %reduce-scatter.20.cloned.1.call-start = ((), (), s32[]{:S(2)}) async-start(), calls=%async_computation.12 | async-start | bytes 2654208 | tf_op jit(solution)/shard_map/reduce_scatter | solution.py:305
  290.5 45.9 %copy-start.78 = (f32[768]{0:T(1024)S(1)}, f32[768]{0:T(1024)}, u32[]{:S(2)}) copy-start(f32[768]{0:T(1024)} %param.17) | copy-start | bytes 9220
  290.5 45.9 %copy-start.90 = (f32[128]{0:T(128)S(1)}, f32[128]{0:T(128)}, u32[]{:S(2)}) copy-start(f32[128]{0:T(128)} %copy-done.89) | copy-start | bytes 1540
  290.5 47.1 %copy-start.105 = (f32[128]{0:T(128)S(1)}, f32[128]{0:T(128)}, u32[]{:S(2)}) copy-start(f32[128]{0:T(128)} %copy-done.104) | copy-start | bytes 1540
  290.5 47.1 %copy-start.99 = (f32[128]{0:T(128)S(1)}, f32[128]{0:T(128)}, u32[]{:S(2)}) copy-start(f32[128]{0:T(128)} %copy-done.98) | copy-start | bytes 1540
  290.5 89.3 %copy-start.28 = (f32[1,128,768]{2,1,0:T(8,128)S(1)}, f32[1,128,768]{2,1,0:T(8,128)}, u32[]{:S(2)}) copy-start(f32[1,128,768]{2,1,0:T(8,128)} %copy-done.27) | copy-start | bytes 1179652
  290.5 89.3 %copy-start.51 = (bf16[1,128,768]{2,1,0:T(8,128)(2,1)S(1)}, bf16[1,128,768]{2,1,0:T(8,128)(2,1)}, u32[]{:S(2)}) copy-start(bf16[1,128,768]{2,1,0:T(8,128)(2,1)} %param.25) | copy-start | bytes 589828
  290.5 89.3 %copy-start.102 = (f32[128]{0:T(128)S(1)}, f32[128]{0:T(128)}, u32[]{:S(2)}) copy-start(f32[128]{0:T(128)} %copy-done.101) | copy-start | bytes 1540
  290.6 265.1 %copy-start.1 = (bf16[768,768]{1,0:T(8,128)(2,1)S(1)}, bf16[768,768]{1,0:T(8,128)(2,1)}, u32[]{:S(2)}) copy-start(bf16[768,768]{1,0:T(8,128)(2,1)} %param.23) | copy-start | bytes 3538948
  (93 other events, 297.5 us)
Sparse Core Ops, SparseCore 0:
  85.2 23.1 reduce-scatter.11
  127.2 23.6 reduce-scatter.15
  153.4 23.2 reduce-scatter.13
  247.0 64.7 reduce-scatter.25
  314.2 22.2 reduce-scatter.17
  340.7 69.8 reduce-scatter.21
  415.1 67.9 reduce-scatter.23
  487.6 67.9 reduce-scatter.19
where the time goes:
time: 570 us; the launch traced here: 563 us
  waiting for transfers between devices  274 us (48%)
  matrix products  91.8 us (16%)
  blocking collectives  77.1 us (14%)
  local copies, waits for them, and re-layouts  55.3 us (10%)
  other arithmetic  33.6 us (6%)
  between operations  16 us (3%)
  starting transfers between devices  15.1 us (3%)
    reduce_scatter x1, waiting for transfers between devices, per_device(): lax.psum_scatter(grad_down, ('seq', 'batch'), scatter_dimension=1, tiled=...  72.5 us
    reduce_scatter x1, waiting for transfers between devices, per_device(): lax.psum_scatter(grad_qkv_weight, ('seq', 'batch'), scatter_dimension=0,...  72.5 us
    unnamed x1, blocking collectives  40.4 us
    reduce_scatter x1, waiting for transfers between devices, per_device(): lax.psum_scatter(grad_up, ('seq', 'batch'), scatter_dimension=0, tiled=True)  28.9 us
    reduce_scatter x1, waiting for transfers between devices, per_device(): lax.psum_scatter(jnp.einsum('stce,dce->std', grad_qkv, w_qkv, preferred_e...  23 us
    reduce_scatter x1, waiting for transfers between devices, per_device(): lax.psum_scatter(down_term.astype(jnp.bfloat16), 'head', scatter_dimensio...  22.9 us
    unnamed x9, waiting for transfers between devices  20.7 us
    reduce_scatter x1, waiting for transfers between devices, per_device(): lax.psum_scatter(jnp.einsum('stf,df->std', grad_upper, w_up, preferred_el...  19.6 us
  transfers between devices with their start and end apart: 16, of which 9 were waited for; matrix products, arithmetic and copies ran while one was open for 14% of the time, Pallas kernels for 0%

commit v1 on v0

v1 whole, which is shorter than its diff:
```python
import functools
import math
from types import SimpleNamespace

import jax
import jax.numpy as jnp
from jax import lax
from jax.experimental import pallas as pl
from jax.experimental.pallas import tpu as pltpu
from jax.sharding import PartitionSpec as P

DH = 64
BLK = 64
LANES = 128
TILE = 128
STATE = 80
F32 = jnp.float32
BF16 = jnp.bfloat16
MESH = pl.DeviceIdType.MESH


def nn(a, b):
    return lax.dot_general(a, b, (((1,), (0,)), ((), ())), preferred_element_type=F32)


def nt(a, b):
    return lax.dot_general(a, b, (((1,), (1,)), ((), ())), preferred_element_type=F32)


def tn(a, b):
    return lax.dot_general(a, b, (((0,), (0,)), ((), ())), preferred_element_type=F32)


def normalize(x):
    center = x - jnp.mean(x, axis=-1, keepdims=True)
    rstd = lax.rsqrt(jnp.mean(center * center, axis=-1, keepdims=True) + 1e-05)
    return center * rstd, rstd


def norm_back(grad, gain, xhat, rstd):
    g = grad * gain
    return rstd * (
        g - jnp.mean(g, axis=-1, keepdims=True) - xhat * jnp.mean(g * xhat, axis=-1, keepdims=True)
    )


def gelu_both(u):
    k0 = math.sqrt(2.0 / math.pi)
    u2 = u * u
    th = jnp.tanh(k0 * (u + 0.044715 * u2 * u))
    half = 0.5 * (1.0 + th)
    slope = half + 0.5 * u * (1.0 - th * th) * (k0 * (1.0 + 3.0 * 0.044715 * u2))
    return u * half, slope


class Plan:
    def __init__(self):
        self.shapes = []
        self.tree = {}

    def add(self, into=None, **buffers):
        into = self.tree if into is None else into
        for name, (shape, dtype) in buffers.items():
            into[name] = len(self.shapes)
            self.shapes.append(pltpu.VMEM(shape, dtype))

    def group(self, **groups):
        for name, buffers in groups.items():
            self.tree[name] = {}
            self.add(self.tree[name], **buffers)

    def semaphores(self, **counts):
        for name, n in counts.items():
            self.tree[name] = len(self.shapes)
            self.shapes.append(pltpu.SemaphoreType.DMA((n,)))

    def bind(self, refs):
        def walk(tree):
            return SimpleNamespace(
                **{k: walk(v) if isinstance(v, dict) else refs[v] for k, v in tree.items()}
            )

        return walk(self.tree)


def make_kernel(dims, n_in, n_out, plan):
    nh, ns, nb, T, R, D, E, FL, H, M, inner = dims
    nt_tiles = T // TILE
    half_rows = D // ns
    piece = D // (ns * nb)

    def kernel(*refs):
        (
            tok_hbm, seg_ref, pat_ref, omega_ref, g1_ref, b1_ref, wqkv_hbm, wout_hbm,
            g2_ref, b2_ref, wup_hbm, wdown_hbm, og_hbm,
        ) = refs[:n_in]
        (
            mixed_ref, gtok_ref, norm_ref, oqkv_ref, oout_ref, oup_ref, odown_ref,
        ) = refs[n_in : n_in + n_out]
        s = plan.bind(refs[n_in + n_out :])
        ssem, rsem, lsem = s.ssem, s.rsem, s.lsem
        used = {"r": 0, "l": 0}
        sends = []

        head = lax.axis_index("head")
        seq = lax.axis_index("seq")
        bat = lax.axis_index("batch")
        h1 = head + 1 - 2 * lax.rem(head, 2)
        h2 = lax.rem(head + 2, nh)
        h3 = lax.rem(h1 + 2, nh)
        other = 1 - seq

        def local(src, dst):
            k = used["l"]
            used["l"] += 1
            c = pltpu.make_async_copy(src, dst, lsem.at[k])
            c.start()
            return c

        def send(src, dst, **dev):
            k = used["r"]
            used["r"] += 1
            c = pltpu.make_async_remote_copy(
                src_ref=src, dst_ref=dst, send_sem=ssem.at[k], recv_sem=rsem.at[k],
                device_id=dev, device_id_type=MESH,
            )
            c.start()
            sends.append(c)
            return c

        def rows(slot, n=TILE):
            return pl.ds(pl.multiple_of(slot * n, n), n)

        c_tok = local(tok_hbm.at[0], s.tok.at[head])
        c_wqkv = local(wqkv_hbm, s.wqkv)
        c_wout = local(wout_hbm, s.wo.at[head])
        c_og = local(og_hbm.at[0], s.og.at[head])
        c_wup = local(wup_hbm, s.wup)
        c_wdown = local(wdown_hbm, s.wdown)
        barrier = pltpu.get_barrier_semaphore()
        peers = [dict(head=h1), dict(head=h2), dict(head=h3), dict(seq=other)]
        if inner:
            peers += [dict(batch=lax.rem(bat + d, nb)) for d in range(1, nb)]
        for dev in peers:
            pl.semaphore_signal(barrier, inc=1, device_id=dev, device_id_type=MESH)
        pl.semaphore_wait(barrier, len(peers))

        def gather_start(buf, chunks):
            n = buf.shape[1] // chunks
            out = []
            for i in range(chunks):
                part = buf.at[head, pl.ds(i * n, n)]
                across = send(part, part, head=h2)
                beside = send(part, part, head=h1)
                out.append((across, beside, i * n, n))
            return out

        def gather_forward(buf, started):
            out = []
            for across, _, lo, n in started:
                across.wait_recv()
                part = buf.at[h2, pl.ds(lo, n)]
                out.append(send(part, part, head=h1))
            return out

        c_tok.wait()
        ag_tok = gather_start(s.tok, 2)

        lane = lax.broadcasted_iota(jnp.int32, (1, LANES), 1)
        low = lane < DH
        ones_lanes = ((lane == DH) | (lane == DH + 1)).astype(F32)
        seg_all = seg_ref[...].astype(F32)
        first = seq == 0
        seg_half = jnp.where(first, seg_all[:, :T], seg_all[:, T : 2 * T])
        seg_prev = jnp.where(first, -1.0, seg_all[:, T - BLK : T])
        tail_one = jnp.where(first, -1.0, jnp.broadcast_to(seg_all[:, T - 1 : T], (1, LANES)))
        tail_two = jnp.where(
            first, -1.0, jnp.broadcast_to(seg_all[:, T - BLK - 1 : T - BLK], (1, LANES))
        )
        s.segrow[...] = jnp.broadcast_to(seg_half, (8, T))
        s.segcol[...] = jnp.transpose(jnp.broadcast_to(seg_half, (LANES, T)))
        segcol = s.segcol[...]
        row_id = lax.broadcasted_iota(jnp.int32, (T, LANES), 0)
        mask_one = (segcol == segcol[T - 1 : T, :]).astype(F32)
        mask_two = ((segcol == segcol[T - BLK - 1 : T - BLK, :]) & (row_id < T - BLK)).astype(F32)
        s.m1[...] = mask_one
        s.m0[...] = mask_two
        s.mfar[...] = jnp.where(
            row_id < BLK, (segcol == tail_two).astype(F32), (segcol == tail_one).astype(F32)
        )
        nblk = pat_ref.shape[1]
        per_half = T // BLK
        hot = (
            lax.broadcasted_iota(jnp.int32, (T, nblk), 1)
            == lax.broadcasted_iota(jnp.int32, (T, nblk), 0) // BLK + seq * per_half
        ).astype(F32)
        pat = pat_ref[...].astype(F32)
        for h in range(H):
            s.thr[h] = 3.0 - nn(
                (hot * pat[h : h + 1, :]).astype(BF16), jnp.ones((nblk, LANES), BF16)
            )
        wrow = lax.broadcasted_iota(jnp.int32, (TILE, 2 * TILE), 0)
        wcol = lax.broadcasted_iota(jnp.int32, (TILE, 2 * TILE), 1)
        dist = 2 + wrow // BLK - wcol // BLK
        kind = jnp.where(
            dist >= 2,
            1.0,
            jnp.where(dist == 1, 2.0, jnp.where((dist == 0) & (wcol - TILE <= wrow), 3.0, 0.0)),
        )
        for t in range(nt_tiles):
            col = segcol[t * TILE : (t + 1) * TILE, :]
            for side in range(2):
                tile = t - 1 + side
                if tile < 0:
                    continue
                same = col == s.segrow[0:1, tile * TILE : (tile + 1) * TILE]
                s.code[t, :, side * TILE : (side + 1) * TILE] = jnp.where(
                    same, kind[:, side * TILE : (side + 1) * TILE], 0.0
                )
        scale = DH ** (-0.25)
        om = omega_ref[...] * scale
        om_high = om.astype(BF16)
        s.omst[0:DH, :] = om_high
        s.omst[DH : 2 * DH, :] = (om - om_high.astype(F32)).astype(BF16)
        s.omtmp[...] = jnp.zeros((LANES, M), F32)
        s.omtmp[0:DH, :] = om
        s.omtmp[DH : DH + 8, :] = (
            lax.broadcasted_iota(jnp.int32, (8, M), 0) == 0
        ).astype(F32)
        s.omt[...] = jnp.transpose(s.omtmp[...]).astype(BF16)
        c_wqkv.wait()
        for c in range(3):
            for h in range(H):
                src = s.wqkv[c * E + h * DH : c * E + (h + 1) * DH, :]
                base = (c * H + h) * LANES
                s.wpad[base : base + DH, :] = src
                s.wpad[base + DH : base + 2 * DH, :] = src if c < 2 else jnp.zeros_like(src)
        c_wout.wait()
        for h in range(H):
            s.wopad[h * LANES : h * LANES + DH, :] = s.wo[head, h * DH : (h + 1) * DH, :]
            s.wopad[h * LANES + DH : (h + 1) * LANES, :] = jnp.zeros((DH, D), BF16)
        for h in range(H):
            for i in range(2):
                s.rin[h, i, STATE:LANES, :] = jnp.zeros((LANES - STATE, M), BF16)
                s.grin[h, i, STATE:LANES, :] = jnp.zeros((LANES - STATE, M), BF16)

        def features(twice):
            x = twice.astype(F32)
            square = jnp.sum(x * x, axis=-1, keepdims=True)
            projected = nn(twice, s.omst[...])
            return jnp.exp(projected - square * (scale * scale * 0.25)) * (1.0 / math.sqrt(M))

        gain1, bias1 = g1_ref[...], b1_ref[...]
        gain2, bias2 = g2_ref[...], b2_ref[...]

        def project(slot):
            xhat, _ = normalize(s.tok[slot].astype(F32))
            normed = (xhat * gain1 + bias1).astype(BF16)
            at = rows(slot)
            s.n1[at, :] = normed
            for c in range(3):
                out = nt(normed, s.wpad[c * H * LANES : (c + 1) * H * LANES, :])
                for h in range(H):
                    part = out[:, h * LANES : (h + 1) * LANES]
                    if c == 2:
                        s.v[h, at, :] = (part + ones_lanes).astype(BF16)
                    else:
                        low_part = part.astype(BF16)
                        (s.q, s.k)[c][h, at, :] = low_part
                        (s.fq, s.fk)[c][h, at, :] = features(low_part).astype(BF16)

        project(head)
        for _, beside, _, _ in ag_tok:
            beside.wait_recv()
        project(h1)
        fw_tok = gather_forward(s.tok, ag_tok)
        ag_wo = gather_start(s.wo, 1)
        project(h2)
        for c in fw_tok:
            c.wait_recv()
        project(h3)

        for h in range(H):
            fk = s.fk[h]
            v = s.v[h].astype(F32)
            v1 = (v * s.m1[...]).astype(BF16)
            v0 = (v * s.m0[...]).astype(BF16)
            s.v1[h] = v1
            s.v0[h] = v0
            s.rout[h, 0] = tn(v0, fk)[:STATE].astype(BF16)
            s.rout[h, 1] = tn(v1, fk)[:STATE].astype(BF16)
            kk = s.k[h, T - BLK : T, :].astype(F32)
            vv = v[T - BLK : T, :]
            s.kvout[h] = jnp.where(low, kk, pltpu.roll(vv, DH, 1)).astype(BF16)
        ex_kv = send(s.kvout, s.kvin, seq=other)
        ex_r = [
            send(s.rout.at[h], s.rin.at[h, :, pl.ds(0, STATE)], seq=other) for h in range(H)
        ]

        def attend(h, carry):
            for t in range(nt_tiles):
                lo, hi = t * TILE, (t + 1) * TILE
                w0 = max(0, lo - TILE)
                fq = s.fq[h, lo:hi, :]
                low_rank = nt(fq, s.fk[h, 0:hi, :])
                exact = jnp.exp(nt(s.q[h, lo:hi, :], s.k[h, w0:hi, :]) * (0.5 / math.sqrt(DH)))
                tiles = (hi - w0) // TILE
                code = s.code[t, :, (2 - tiles) * TILE :]
                thr = jnp.concatenate([s.thr[h, lo:hi, :]] * tiles, axis=1)
                near = jnp.where(
                    code >= thr, exact, jnp.where(code >= 1.0, low_rank[:, w0:], 0.0)
                )
                if w0 > 0:
                    col = jnp.concatenate([s.segcol[lo:hi, :]] * (w0 // TILE), axis=1)
                    far = jnp.where(col == s.segrow[0:1, 0:w0], low_rank[:, :w0], 0.0)
                    near = jnp.concatenate([far, near], axis=1)
                w = near.astype(BF16)
                s.w[h, lo:hi, 0:hi] = w
                s.acc[h, lo:hi, :] = nn(w, s.v[h, 0:hi, :])
            return carry

        lax.fori_loop(0, H, attend, 0)
        fw_wo = gather_forward(s.wo, ag_wo)
        c_og.wait()
        ag_og = gather_start(s.og, 1)

        ex_kv.wait_recv()
        for c in ex_r:
            c.wait_recv()

        def unpack(packed):
            x = packed.astype(F32)
            turned = pltpu.roll(x, DH, 1)
            twice = jnp.where(low, x, turned).astype(BF16)
            return twice, jnp.where(low, turned, 0.0)

        same_in = s.segcol[0:BLK, 0:BLK] == seg_prev
        for h in range(H):
            k_in, v_in = unpack(s.kvin[h])
            v_in = (v_in + ones_lanes).astype(BF16)
            f_in = features(k_in).astype(BF16)
            s.kin[h] = k_in
            s.vin[h] = v_in
            s.fin[h] = f_in
            q0 = s.q[h, 0:BLK, :]
            fq0 = s.fq[h, 0:BLK, :]
            exact = jnp.exp(nt(q0, k_in) * (0.5 / math.sqrt(DH)))
            low_rank = nt(fq0, f_in)
            use_exact = s.thr[h, 0:BLK, 0:BLK] < 2.5
            w_in = jnp.where(same_in, jnp.where(use_exact, exact, low_rank), 0.0).astype(BF16)
            s.win[h] = w_in
            far0 = jnp.where(
                s.mfar[0:BLK, :] > 0.5, nt(fq0, s.rin[h, 0]), 0.0
            )
            s.acc[h, 0:BLK, :] = s.acc[h, 0:BLK, :] + nn(w_in, v_in) + far0
            far1 = jnp.where(
                s.mfar[BLK:T, :] > 0.5, nt(s.fq[h, BLK:T, :], s.rin[h, 1]), 0.0
            )
            s.acc[h, BLK:T, :] = s.acc[h, BLK:T, :] + far1

        def divided(h, lo, hi):
            acc = s.acc[h, lo:hi, :]
            inv = 1.0 / acc[:, DH : DH + 1]
            return acc * inv, inv

        ag_at = []
        fw_at = []
        for t in range(nt_tiles):
            lo, hi = t * TILE, (t + 1) * TILE
            outs = [divided(h, lo, hi)[0] for h in range(H)]
            for h in range(0, H, 2):
                if h + 1 < H:
                    both = jnp.where(low, outs[h], pltpu.roll(outs[h + 1], DH, 1))
                    s.at[head, lo:hi, h * DH : (h + 2) * DH] = both.astype(BF16)
                else:
                    s.at[head, lo:hi, h * DH : (h + 1) * DH] = outs[h][:, :DH].astype(BF16)
            part = s.at.at[head, pl.ds(lo, TILE)]
            ag_at.append((send(part, part, head=h2), send(part, part, head=h1), lo, TILE))
        for c in fw_wo:
            c.wait_recv()
        for _, c, _, _ in ag_wo:
            c.wait_recv()
        fw_at = gather_forward(s.at, ag_at)
        fw_og = gather_forward(s.og, ag_og)
        for _, c, _, _ in ag_og:
            c.wait_recv()
        for c in fw_og:
            c.wait_recv()
        for _, c, _, _ in ag_at:
            c.wait_recv()
        for c in fw_at:
            c.wait_recv()
        c_wup.wait()
        c_wdown.wait()

        def scatter_sum(make, bufs):
            out, got = bufs.out, bufs.got
            out[0] = make(h3).astype(BF16)
            a = send(out.at[0], got.at[0], head=h1)
            mine = make(h2)
            a.wait_recv()
            out[1] = (mine + got[0].astype(F32)).astype(BF16)
            b = send(out.at[1], got.at[1], head=h2)
            out[2] = make(h1).astype(BF16)
            c = send(out.at[2], got.at[2], head=h1)
            return (b, c)

        def scatter_done(pending, bufs, own):
            got = bufs.got
            b, c = pending
            c.wait_recv()
            b.wait_recv()
            return own + got[1].astype(F32) + got[2].astype(F32)

        def feed(slot):
            at = rows(slot)
            hid = s.tok[slot].astype(F32)
            for j in range(nh):
                hid = hid + nn(s.at[j, at, :], s.wo[j])
            s.hid[at, :] = hid
            xhat, _ = normalize(hid)
            normed = (xhat * gain2 + bias2).astype(BF16)
            s.n2[at, :] = normed
            act, slope = gelu_both(nn(normed, s.wup[...]))
            s.act[at, :] = act.astype(BF16)
            gu = (nt(s.og[slot], s.wdown[...]) * slope).astype(BF16)
            s.gu[at, :] = gu
            return nt(gu, s.wup[...])

        pend = scatter_sum(feed, s.ra)
        own = feed(head)

        def weight_grad(name, left, right):
            a = left(pl.ds(pl.multiple_of(other * half_rows, LANES), half_rows))
            b = right()
            if inner:
                name.ys[...] = tn(a, b).astype(BF16)
                c = send(name.ys, name.yr, seq=other)
                a = left(pl.ds(pl.multiple_of(seq * half_rows, LANES), half_rows))
                name.own[...] = tn(a, b)
                return c
            return None

        def weight_cross(name, c):
            c.wait_recv()
            out = []
            for d in range(1, nb):
                at = rows(lax.rem(bat + d, nb), piece)
                name.zs[d - 1] = (
                    name.own[at, :] + name.yr[at, :].astype(F32)
                ).astype(BF16)
                out.append(
                    send(
                        name.zs.at[d - 1], name.zr.at[d - 1],
                        batch=lax.rem(bat + d, nb),
                    )
                )
            return out

        def weight_sum(name, cs):
            at = rows(bat, piece)
            total = name.own[at, :] + name.yr[at, :].astype(F32)
            for d, c in enumerate(cs):
                c.wait_recv()
                total = total + name.zr[d].astype(F32)
            return total

        def og_cols(at):
            return jnp.concatenate([s.og[j, :, at] for j in range(nh)], axis=0)

        if inner:
            y_down = weight_grad(s.wd, og_cols, lambda: s.act[...])

        grad2 = scatter_done(pend, s.ra, own)
        mine = rows(head)
        xhat2, rstd2 = normalize(s.hid[mine, :])
        s.ns[...] = jnp.zeros_like(s.ns)
        s.ns[2:3, :] = jnp.sum(grad2 * xhat2, axis=0, keepdims=True)
        s.ns[3:4, :] = jnp.sum(grad2, axis=0, keepdims=True)
        grad_hidden = s.og[head].astype(F32) + norm_back(grad2, gain2, xhat2, rstd2)
        s.gh[...] = grad_hidden
        s.gb[head] = grad_hidden.astype(BF16)
        ag_gb = gather_start(s.gb, 2)
        if inner:
            y_up = weight_grad(s.wu, lambda at: s.n2[:, at], lambda: s.gu[...])

        def divide_back(slot):
            at = rows(slot)
            ga = nt(s.gb[slot], s.wopad[...])
            for h in range(H):
                acc = s.acc[h, at, :]
                inv = 1.0 / acc[:, DH : DH + 1]
                gnum = ga[:, h * LANES : (h + 1) * LANES] * inv
                gden = -jnp.sum(gnum * acc, axis=-1, keepdims=True) * inv
                high = gden.astype(BF16).astype(F32)
                gnum = jnp.where(lane == DH, high, jnp.where(lane == DH + 1, gden - high, gnum))
                s.gn[h, at, :] = gnum.astype(BF16)

        divide_back(head)
        for _, c, _, _ in ag_gb:
            c.wait_recv()
        divide_back(h1)
        fw_gb = gather_forward(s.gb, ag_gb)
        divide_back(h2)
        for c in fw_gb:
            c.wait_recv()
        divide_back(h3)

        def feature_back(gfeat, feat, twice):
            x = nn((gfeat * feat.astype(F32)).astype(BF16), s.omt[...])
            return x - twice.astype(F32) * (x[:, DH : DH + 1] * (scale * scale))

        for h in range(H):
            gm = jnp.where(s.mfar[...] > 0.5, s.gn[h].astype(F32), 0.0).astype(BF16)
            s.gm[h] = gm
            s.grout[h, 0] = tn(gm[0:BLK, :], s.fq[h, 0:BLK, :])[:STATE].astype(BF16)
            s.grout[h, 1] = tn(gm[BLK:T, :], s.fq[h, BLK:T, :])[:STATE].astype(BF16)
            gn0 = s.gn[h, 0:BLK, :]
            q0 = s.q[h, 0:BLK, :]
            fq0 = s.fq[h, 0:BLK, :]
            gw = nt(gn0, s.vin[h])
            w_in = s.win[h]
            use_exact = s.thr[h, 0:BLK, 0:BLK] < 2.5
            gs = jnp.where(
                same_in & use_exact, gw * w_in.astype(F32) * (1.0 / math.sqrt(DH)), 0.0
            ).astype(BF16)
            gp = jnp.where(same_in & jnp.logical_not(use_exact), gw, 0.0).astype(BF16)
            gk = feature_back(tn(gp, fq0), s.fin[h], s.kin[h]) + tn(gs, q0)
            gv = tn(w_in, gn0)
            s.gkvout[h] = jnp.where(low, gk, pltpu.roll(gv, DH, 1)).astype(BF16)
            s.gfq0[h] = nn(gp, s.fin[h])
            s.gq0[h] = nn(gs, s.kin[h])
        ex_gkv = send(s.gkvout, s.gkvin, seq=other)
        ex_gr = [
            send(s.grout.at[h], s.grin.at[h, :, pl.ds(0, STATE)], seq=other) for h in range(H)
        ]

        if inner:
            z_down = weight_cross(s.wd, y_down)

        def attend_back(h, carry):
            for t in range(nt_tiles):
                lo, hi = t * TILE, (t + 1) * TILE
                w0 = max(0, lo - TILE)
                tiles = (hi - w0) // TILE
                gw = nt(s.gn[h, lo:hi, :], s.v[h, 0:hi, :])
                code = s.code[t, :, (2 - tiles) * TILE :]
                thr = jnp.concatenate([s.thr[h, lo:hi, :]] * tiles, axis=1)
                use_exact = code >= thr
                near = gw[:, w0:]
                gs = jnp.where(
                    use_exact,
                    near * s.w[h, lo:hi, w0:hi].astype(F32) * (1.0 / math.sqrt(DH)),
                    0.0,
                ).astype(BF16)
                gp = jnp.where((code >= 1.0) & (code < thr), near, 0.0)
                if w0 > 0:
                    col = jnp.concatenate([s.segcol[lo:hi, :]] * (w0 // TILE), axis=1)
                    far = jnp.where(col == s.segrow[0:1, 0:w0], gw[:, :w0], 0.0)
                    gp = jnp.concatenate([far, gp], axis=1)
                gp = gp.astype(BF16)
                s.gp[lo:hi, 0:hi] = gp
                s.gs[lo:hi, (2 - tiles) * TILE :] = gs
                gfq = nn(gp, s.fk[h, 0:hi, :])
                gq = nn(gs, s.k[h, w0:hi, :])
                gm = s.gm[h, lo:hi, :]
                if t == 0:
                    top = nn(gm[0:BLK], s.rin[h, 0]) + s.gfq0[h]
                    bottom = nn(gm[BLK:], s.rin[h, 1])
                    gfq = gfq + jnp.concatenate([top, bottom], axis=0)
                    gq = gq + jnp.concatenate(
                        [s.gq0[h], jnp.zeros((TILE - BLK, LANES), F32)], axis=0
                    )
                else:
                    gfq = gfq + nn(gm, s.rin[h, 1])
                gq = gq + feature_back(gfq, s.fq[h, lo:hi, :], s.q[h, lo:hi, :])
                s.gq[h, lo:hi, :] = gq
            for t in range(nt_tiles):
                lo, hi = t * TILE, (t + 1) * TILE
                s.gfk[h, lo:hi, :] = tn(s.gp[lo:T, lo:hi], s.fq[h, lo:T, :])
                s.gv[h, lo:hi, :] = tn(s.w[h, lo:T, lo:hi], s.gn[h, lo:T, :])
                gk = tn(s.gs[lo:hi, TILE:], s.q[h, lo:hi, :])
                if t + 1 < nt_tiles:
                    gk = gk + tn(s.gs[hi : hi + TILE, :TILE], s.q[h, hi : hi + TILE, :])
                s.gk[h, lo:hi, :] = gk
            return carry

        lax.fori_loop(0, H, attend_back, 0)

        def gb_cols(at):
            return jnp.concatenate([s.gb[j, :, at] for j in range(nh)], axis=0)

        if inner:
            y_out = weight_grad(s.wo_g, gb_cols, lambda: s.at[head])
            z_up = weight_cross(s.wu, y_up)

        ex_gkv.wait_recv()
        for c in ex_gr:
            c.wait_recv()

        def finish(h, carry):
            v1, v0 = s.v1[h], s.v0[h]
            r0 = jnp.where(first, s.grin[h, 0].astype(F32), 0.0).astype(BF16)
            r1 = jnp.where(first, s.grin[h, 1].astype(F32), 0.0).astype(BF16)
            gfk = s.gfk[h] + nn(v0, r0) + nn(v1, r1)
            fk = s.fk[h]
            gv = s.gv[h] + s.m0[...] * nt(fk, r0) + s.m1[...] * nt(fk, r1)
            gk = s.gk[h] + feature_back(gfk, fk, s.k[h])
            s.gk[h] = gk
            s.gv[h] = gv
            back = jnp.where(first, s.gkvin[h].astype(F32), 0.0)
            s.gk[h, T - BLK : T, :] = s.gk[h, T - BLK : T, :] + back
            s.gv[h, T - BLK : T, :] = s.gv[h, T - BLK : T, :] + pltpu.roll(back, DH, 1)
            return carry

        lax.fori_loop(0, H, finish, 0)
        parts = [(n, h) for n in (s.gq, s.gk, s.gv) for h in range(H)]
        for i in range(0, len(parts), 2):
            (na, ha) = parts[i]
            a = na[ha]
            if i + 1 < len(parts):
                (nb_, hb) = parts[i + 1]
                a = jnp.where(low, a, pltpu.roll(nb_[hb], DH, 1))
                s.gqkv[:, i * DH : (i + 2) * DH] = a.astype(BF16)
            else:
                s.gqkv[:, i * DH : (i + 1) * DH] = a[:, :DH].astype(BF16)

        if inner:
            y_qkv = weight_grad(s.wx, lambda at: s.n1[:, at], lambda: s.gqkv[...])

        pend = scatter_sum(lambda slot: nn(s.gqkv[rows(slot), :], s.wqkv[...]), s.rb)
        own = nn(s.gqkv[mine, :], s.wqkv[...])
        if inner:
            z_out = weight_cross(s.wo_g, y_out)

        pend_mixed = scatter_sum(lambda slot: nn(s.act[rows(slot), :], s.wdown[...]), s.rc)
        own_mixed = nn(s.act[mine, :], s.wdown[...])

        grad1 = scatter_done(pend, s.rb, own)
        xhat1, rstd1 = normalize(s.tok[head].astype(F32))
        s.ns[0:1, :] = jnp.sum(grad1 * xhat1, axis=0, keepdims=True)
        s.ns[1:2, :] = jnp.sum(grad1, axis=0, keepdims=True)
        gtok_ref[0] = s.gh[...] + norm_back(grad1, gain1, xhat1, rstd1)

        if inner:
            n_z = [
                send(s.ns, s.nz.at[d - 1], batch=lax.rem(bat + d, nb)) for d in range(1, nb)
            ]
            z_qkv = weight_cross(s.wx, y_qkv)
        mixed_ref[0] = (s.hid[mine, :] + scatter_done(pend_mixed, s.rc, own_mixed)).astype(BF16)

        if inner:
            total = s.ns[...]
            for d, c in enumerate(n_z):
                c.wait_recv()
                total = total + s.nz[d]
            s.ns2[...] = total
            c = send(s.ns2, s.ny, seq=other)
            odown_ref[...] = weight_sum(s.wd, z_down)
            oup_ref[...] = weight_sum(s.wu, z_up)
            c.wait_recv()
            s.ns3[...] = total + s.ny[...]
            n_h = [send(s.ns3, s.nh.at[i], head=d) for i, d in enumerate((h1, h2, h3))]
            s.otmp[...] = jnp.zeros_like(s.otmp)
            s.otmp[0:piece, 0:E] = weight_sum(s.wo_g, z_out)
            oout_ref[...] = jnp.transpose(s.otmp[...])[:E, :piece]
            total = s.ns3[...]
            for i, c in enumerate(n_h):
                c.wait_recv()
                total = total + s.nh[i]
            width = D // (ns * nb * nh)
            start = ((seq * nb + bat) * nh + head) * width
            pick = (
                lax.broadcasted_iota(jnp.int32, (D, LANES), 0)
                == lax.broadcasted_iota(jnp.int32, (D, LANES), 1) + start
            ).astype(F32)
            norm_ref[...] = lax.dot_general(
                total, pick, (((1,), (0,)), ((), ())),
                precision=lax.Precision.HIGHEST, preferred_element_type=F32,
            )
            gx = weight_sum(s.wx, z_qkv)
            for c in range(3):
                oqkv_ref[c] = gx[:, c * E : (c + 1) * E]
        else:
            norm_ref[...] = s.ns[...]
            odown_ref[...] = tn(og_cols(slice(0, D)), s.act[...])
            oup_ref[...] = tn(s.n2[...], s.gu[...])
            oout_ref[...] = tn(gb_cols(slice(0, D)), s.at[head])
            oqkv_ref[...] = tn(s.n1[...], s.gqkv[...])
        for c in sends:
            c.wait_send()

    return kernel


def build(dims):
    nh, ns, nb, T, R, D, E, FL, H, M, inner = dims
    plan = Plan()
    piece = D // (ns * nb)
    half = D // ns
    plan.add(
        tok=((nh, R, D), BF16),
        og=((nh, R, D), BF16),
        wqkv=((3 * E, D), BF16),
        wo=((nh, E, D), BF16),
        wup=((D, FL), BF16),
        wdown=((FL, D), BF16),
        wpad=((3 * H * LANES, D), BF16),
        wopad=((H * LANES, D), BF16),
        segrow=((8, T), F32),
        segcol=((T, LANES), F32),
        m0=((T, LANES), F32),
        m1=((T, LANES), F32),
        mfar=((T, LANES), F32),
        thr=((H, T, LANES), F32),
        code=((T // TILE, TILE, 2 * TILE), F32),
        omst=((2 * DH, M), BF16),
        omtmp=((LANES, M), F32),
        omt=((M, LANES), BF16),
        n1=((T, D), BF16),
        q=((H, T, LANES), BF16),
        k=((H, T, LANES), BF16),
        v=((H, T, LANES), BF16),
        v0=((H, T, LANES), BF16),
        v1=((H, T, LANES), BF16),
        gn=((H, T, LANES), BF16),
        gm=((H, T, LANES), BF16),
        fq=((H, T, M), BF16),
        fk=((H, T, M), BF16),
        rout=((H, 2, STATE, M), BF16),
        grout=((H, 2, STATE, M), BF16),
        rin=((H, 2, LANES, M), BF16),
        grin=((H, 2, LANES, M), BF16),
        kvout=((H, BLK, LANES), BF16),
        kvin=((H, BLK, LANES), BF16),
        gkvout=((H, BLK, LANES), BF16),
        gkvin=((H, BLK, LANES), BF16),
        kin=((H, BLK, LANES), BF16),
        vin=((H, BLK, LANES), BF16),
        fin=((H, BLK, M), BF16),
        win=((H, BLK, BLK), BF16),
        gfq0=((H, BLK, M), F32),
        gq0=((H, BLK, LANES), F32),
        w=((H, T, T), BF16),
        acc=((H, T, LANES), F32),
        at=((nh, T, E), BF16),
        hid=((T, D), F32),
        n2=((T, D), BF16),
        act=((T, FL), BF16),
        gu=((T, FL), BF16),
        gh=((R, D), F32),
        gb=((nh, R, D), BF16),
        gp=((T, T), BF16),
        gs=((T, 2 * TILE), BF16),
        gfk=((H, T, M), F32),
        gq=((H, T, LANES), F32),
        gk=((H, T, LANES), F32),
        gv=((H, T, LANES), F32),
        gqkv=((T, 3 * E), BF16),
        ns=((8, D), F32),
    )
    pair = dict(out=((3, R, D), BF16), got=((3, R, D), BF16))
    plan.group(ra=pair, rb=pair, rc=pair)
    if inner:

        def weight(width):
            return dict(
                ys=((half, width), BF16),
                yr=((half, width), BF16),
                own=((half, width), F32),
                zs=((nb - 1, piece, width), BF16),
                zr=((nb - 1, piece, width), BF16),
            )

        plan.group(wd=weight(FL), wu=weight(FL), wo_g=weight(E), wx=weight(3 * E))
        plan.add(
            ns2=((8, D), F32),
            ns3=((8, D), F32),
            nz=((nb - 1, 8, D), F32),
            ny=((8, D), F32),
            nh=((3, 8, D), F32),
            otmp=((LANES, 2 * LANES), F32),
        )
    plan.semaphores(ssem=96, rsem=96, lsem=8)

    if inner:
        grads = [(3, piece, E), (E, piece), (piece, FL), (piece, FL)]
        norm = (8, LANES)
    else:
        grads = [(D, 3 * E), (D, E), (D, FL), (D, FL)]
        norm = (8, D)
    outs = [((1, R, D), BF16), ((1, R, D), F32), (norm, F32)] + [(g, F32) for g in grads]
    hbm = pl.BlockSpec(memory_space=pl.ANY)
    vmem = pl.BlockSpec(memory_space=pltpu.VMEM)
    in_specs = [hbm, vmem, vmem, vmem, vmem, vmem, hbm, hbm, vmem, vmem, hbm, hbm, hbm]
    kernel = make_kernel(dims, len(in_specs), len(outs), plan)
    return pl.pallas_call(
        kernel,
        out_shape=[jax.ShapeDtypeStruct(shape, dtype) for shape, dtype in outs],
        in_specs=in_specs,
        out_specs=[vmem] * len(outs),
        scratch_shapes=plan.shapes,
        compiler_params=pltpu.CompilerParams(
            collective_id=0, has_side_effects=True, vmem_limit_bytes=60 << 20
        ),
        name="block",
    )


def per_device(
    mesh_shape,
    tokens,
    seg_ids,
    pattern,
    omega,
    norm1_gain,
    norm1_bias,
    w_qkv,
    w_out,
    norm2_gain,
    norm2_bias,
    w_up,
    w_down,
    out_grad,
):
    nh, ns, nb = mesh_shape
    rows, D = tokens.shape[1:]
    T = seg_ids.shape[1] // ns
    E = w_qkv.shape[2]
    FL = w_up.shape[1]
    piece = D // (ns * nb)
    inner = piece % 16 == 0
    dims = (nh, ns, nb, T, rows, D, E, FL, E // DH, omega.shape[1], inner)
    w_flat = jnp.transpose(w_qkv, (1, 2, 0)).reshape(3 * E, D)
    row = lambda a: a.reshape(1, D)
    mixed, grad_tokens, norms, g_qkv, g_out, g_up, g_down = build(dims)(
        tokens, seg_ids, pattern, omega, row(norm1_gain), row(norm1_bias), w_flat, w_out,
        row(norm2_gain), row(norm2_bias), w_up, w_down, out_grad,
    )
    if inner:
        width = D // (ns * nb * nh)
        norms = norms[:, :width]
        g_qkv = jnp.transpose(g_qkv, (1, 0, 2))
        g_down = g_down.T
    else:
        group = ("seq", "batch")
        scatter = functools.partial(lax.psum_scatter, scatter_dimension=0, tiled=True)
        norms = lax.psum_scatter(
            norms[:4], ("seq", "batch", "head"), scatter_dimension=1, tiled=True
        )
        g_qkv = scatter(g_qkv, group).reshape(piece, 3, E)
        g_out = scatter(g_out, group).T
        g_up = scatter(g_up, group)
        g_down = scatter(g_down, group).T
    return (
        mixed, grad_tokens, norms[0], norms[1], g_qkv, g_out, norms[2], norms[3], g_up, g_down,
    )


def solution(mesh):
    placed = (
        P("batch", ("seq", "head"), None),
        P("batch", None),
        P("head", None),
        P(),
        P(),
        P(),
        P(None, None, "head"),
        P("head", None),
        P(),
        P(),
        P(None, "head"),
        P("head", None),
        P("batch", ("seq", "head"), None),
    )
    shape = (mesh.shape["head"], mesh.shape["seq"], mesh.shape["batch"])
    return jax.shard_map(
        functools.partial(per_device, shape),
        mesh=mesh,
        in_specs=placed,
        out_specs=(
            P("batch", ("seq", "head"), None),
            P("batch", ("seq", "head"), None),
            P(("seq", "batch", "head")),
            P(("seq", "batch", "head")),
            P(("seq", "batch"), None, "head"),
            P("head", ("seq", "batch")),
            P(("seq", "batch", "head")),
            P(("seq", "batch", "head")),
            P(("seq", "batch"), "head"),
            P("head", ("seq", "batch")),
        ),
        check_vma=False,
    )
```

time: 570 us -> 115 us (0.20); the launches traced: 563 us -> 115 us
  waiting for transfers between devices: 274 us -> 0 us
  Pallas kernels: 0 us -> 102 us
  matrix products: 91.8 us -> 0 us
  blocking collectives: 77.1 us -> 0 us
  local copies, waits for them, and re-layouts: 55.3 us -> 12.7 us
  other arithmetic: 33.6 us -> 0 us
  between operations: 16 us -> 0.68 us
  starting transfers between devices: 15.1 us -> 0 us
    reduce_scatter x7 -> x0, waiting for transfers between devices: 253 us -> none  [the longest x1 72.5 us: per_device(): lax.psum_scatter(grad_down, ('seq', 'batch'), scatter_dimension=1, tiled=...]
    pallas_call x0 -> x1, Pallas kernels: none -> 102 us  [per_device(): build(dims)]
    dot_general x42 -> x0, matrix products: 89.7 us -> none  [the longest x7 18 us: feature_map(): jnp.einsum('...td,dm->...tm', scaled, omega, precision=lax.Precision.HIGH...]
    unnamed x1 -> x0, blocking collectives: 40.4 us -> none
    all_gather x4 -> x0, blocking collectives: 36.7 us -> none  [the longest x1 10.1 us: per_device(): grad_rows = lax.all_gather(out_grad, 'head', axis=1, tiled=True)]
    unnamed x9 -> x0, waiting for transfers between devices: 20.7 us -> none
    reduce_sum x18 -> x0, other arithmetic: 16.5 us -> none  [the longest x3 4.16 us: layer_norm(): center = values - jnp.mean(values, axis=-1, keepdims=True)]
    ppermute x8 -> x0, starting transfers between devices: 14.6 us -> none  [shifted(): lax.ppermute(value, axis, [(source, source + steps) for source in range(f...]
  transfers between devices with their start and end apart: 16 -> 0, of which waited for: 9 -> 0; matrix products, arithmetic and copies ran while one was open for 14% -> 0% of each run, Pallas kernels for 0% -> 0%
where the time goes in v1:
time: 115 us
  Pallas kernels  102 us (89%)
  local copies, waits for them, and re-layouts  12.7 us (11%)
    pallas_call x1, Pallas kernels, per_device(): build(dims)  102 us
    unnamed x14, local copies, waits for them, and re-layouts  6.22 us
    reshape x4, local copies, waits for them, and re-layouts, per_device(): row = lambda a: a.reshape(1, D)  5.07 us

profile of v1, /device:TPU:0, one launch (start us, length us, event | category | flops | bytes accessed | tf_op | source)
XLA Modules:
  0.0 114.9 jit_solution(5979204894611885158)
XLA Ops:
  0.6 1.3 %reshape.35.refs_4_ = f32[1,768]{1,0:T(1,128)} reshape(f32[768]{0:T(1024)} %param.17) | data formatting | bytes 6144 | tf_op jit(solution)/shard_map/reshape | solution.py:835
  1.9 1.3 %reshape.36.refs_5_ = f32[1,768]{1,0:T(1,128)} reshape(f32[768]{0:T(1024)} %param.18) | data formatting | bytes 6144 | tf_op jit(solution)/shard_map/reshape | solution.py:835
  3.2 1.3 %reshape.38.refs_8_ = f32[1,768]{1,0:T(1,128)} reshape(f32[768]{0:T(1024)} %param.21) | data formatting | bytes 6144 | tf_op jit(solution)/shard_map/reshape | solution.py:835
  4.4 1.3 %reshape.39.refs_9_ = f32[1,768]{1,0:T(1,128)} reshape(f32[768]{0:T(1024)} %param.22) | data formatting | bytes 6144 | tf_op jit(solution)/shard_map/reshape | solution.py:835
  5.7 101.6 %block.1 = (bf16[1,128,768]{2,1,0:T(8,128)(2,1)}, f32[1,128,768]{2,1,0:T(8,128)}, f32[8,128]{1,0:T(8,128)}, f32[3,96,192]{2,1,0:T(8,128)}, f32[192,96]{1,0:T(8,1...) custom-call(bf16[1,128,768]{2,1,0:T(8,128)(2,1)} %refs_0_.1, s32[1,1024]{1,0:T(1,128)} %refs_1_.1, s32[3,16]{1,0:T(4,128)} %refs_2_.1, ...), custom_call_target="tpu_custom_call" | custom-call | tf_op jit(solution)/shard_map/block/pallas_call | solution.py:836
  107.3 0.0 copy-start.2
  107.3 0.0 copy-start.3
  107.3 0.0 copy-start.1
  107.3 1.4 %slice_bitcast_fusion = (f32[24]{0:T(128)}, f32[24]{0:T(128)}, f32[24]{0:T(128)}, f32[24]{0:T(128)}) fusion(f32[8,128]{1,0:T(8,128)} %get-tuple-element.19), kind=kLoop, calls=%fused_computation | loop fusion | bytes 768 | tf_op jit(solution)/shard_map/squeeze | solution.py:856
  108.7 1.6 %copy.29 = bf16[1,128,768]{2,1,0:T(8,128)(2,1)} copy(bf16[1,128,768]{2,1,0:T(8,128)(2,1)} %get-tuple-element.38) | data formatting | bytes 393216
  110.3 0.0 copy-start
  110.3 1.8 %copy.30 = f32[1,128,768]{2,1,0:T(8,128)} copy(f32[1,128,768]{2,1,0:T(8,128)} %get-tuple-element.39) | data formatting | bytes 786432
  112.1 0.0 copy-done.2
  112.1 0.7 copy.31
  112.8 0.0 copy-done.3
  112.8 0.6 copy.32
  113.5 0.0 copy-done.1
  113.5 0.7 copy.33
  114.2 0.0 copy-done
  114.2 0.7 copy.34
Async XLA Ops:
  107.3 4.8 %copy-start.2 = (f32[3,96,192]{2,1,0:T(8,128)S(1)}, f32[3,96,192]{2,1,0:T(8,128)}, u32[]{:S(2)}) copy-start(f32[3,96,192]{2,1,0:T(8,128)} %get-tuple-element.20) | copy-start | bytes 663556
  107.3 5.5 %copy-start.3 = (f32[192,96]{1,0:T(8,128)S(1)}, f32[192,96]{1,0:T(8,128)}, u32[]{:S(2)}) copy-start(f32[192,96]{1,0:T(8,128)} %get-tuple-element.43) | copy-start | bytes 221188
  107.3 6.2 %copy-start.1 = (f32[96,768]{1,0:T(8,128)S(1)}, f32[96,768]{1,0:T(8,128)}, u32[]{:S(2)}) copy-start(f32[96,768]{1,0:T(8,128)} %get-tuple-element.46) | copy-start | bytes 884740
  110.3 3.9 %copy-start = (f32[96,768]{1,0:T(8,128)S(1)}, f32[96,768]{1,0:T(8,128)}, u32[]{:S(2)}) copy-start(f32[96,768]{1,0:T(8,128)} %get-tuple-element.23) | copy-start | bytes 884740

commit v2 on v1

--- a/solution.py
+++ b/solution.py
@@ -181,9 +181,11 @@
         s.segcol[...] = jnp.transpose(jnp.broadcast_to(seg_half, (LANES, T)))
         segcol = s.segcol[...]
         row_id = lax.broadcasted_iota(jnp.int32, (T, LANES), 0)
-        mask_one = (segcol == segcol[T - 1 : T, :]).astype(F32)
         mask_two = ((segcol == segcol[T - BLK - 1 : T - BLK, :]) & (row_id < T - BLK)).astype(F32)
-        s.m1[...] = mask_one
+        prev_col = jnp.transpose(jnp.broadcast_to(seg_prev, (LANES, BLK)))
+        s.mprev[...] = (prev_col == tail_one).astype(F32)
+        link = (tail_one == tail_two).astype(F32)
+        s.link[...] = jnp.broadcast_to(jnp.concatenate([link] * (M // LANES), axis=1), (8, M))
         s.m0[...] = mask_two
         s.mfar[...] = jnp.where(
             row_id < BLK, (segcol == tail_two).astype(F32), (segcol == tail_one).astype(F32)
@@ -240,9 +242,8 @@
             s.wopad[h * LANES : h * LANES + DH, :] = s.wo[head, h * DH : (h + 1) * DH, :]
             s.wopad[h * LANES + DH : (h + 1) * LANES, :] = jnp.zeros((DH, D), BF16)
         for h in range(H):
-            for i in range(2):
-                s.rin[h, i, STATE:LANES, :] = jnp.zeros((LANES - STATE, M), BF16)
-                s.grin[h, i, STATE:LANES, :] = jnp.zeros((LANES - STATE, M), BF16)
+            s.rin[h, STATE:LANES, :] = jnp.zeros((LANES - STATE, M), BF16)
+            s.grin[h, STATE:LANES, :] = jnp.zeros((LANES - STATE, M), BF16)
 
         def features(twice):
             x = twice.astype(F32)
@@ -250,8 +251,8 @@
             projected = nn(twice, s.omst[...])
             return jnp.exp(projected - square * (scale * scale * 0.25)) * (1.0 / math.sqrt(M))
 
-        gain1, bias1 = g1_ref[...], b1_ref[...]
-        gain2, bias2 = g2_ref[...], b2_ref[...]
+        gain1, bias1 = g1_ref[...].reshape(1, D), b1_ref[...].reshape(1, D)
+        gain2, bias2 = g2_ref[...].reshape(1, D), b2_ref[...].reshape(1, D)
 
         def project(slot):
             xhat, _ = normalize(s.tok[slot].astype(F32))
@@ -283,19 +284,16 @@
         for h in range(H):
             fk = s.fk[h]
             v = s.v[h].astype(F32)
-            v1 = (v * s.m1[...]).astype(BF16)
             v0 = (v * s.m0[...]).astype(BF16)
-            s.v1[h] = v1
             s.v0[h] = v0
-            s.rout[h, 0] = tn(v0, fk)[:STATE].astype(BF16)
-            s.rout[h, 1] = tn(v1, fk)[:STATE].astype(BF16)
+            s.rout[h] = tn(v0, fk)[:STATE].astype(BF16)
             kk = s.k[h, T - BLK : T, :].astype(F32)
             vv = v[T - BLK : T, :]
             s.kvout[h] = jnp.where(low, kk, pltpu.roll(vv, DH, 1)).astype(BF16)
         ex_kv = send(s.kvout, s.kvin, seq=other)
-        ex_r = [
-            send(s.rout.at[h], s.rin.at[h, :, pl.ds(0, STATE)], seq=other) for h in range(H)
-        ]
+        ex_r = send(s.rout, s.rin.at[:, pl.ds(0, STATE)], seq=other)
+        c_og.wait()
+        ag_og = gather_start(s.og, 1)
 
         def attend(h, carry):
             for t in range(nt_tiles):
@@ -321,12 +319,14 @@
 
         lax.fori_loop(0, H, attend, 0)
         fw_wo = gather_forward(s.wo, ag_wo)
-        c_og.wait()
-        ag_og = gather_start(s.og, 1)
+
+        if inner:
+            for j in range(nh):
+                lo = j * TILE
+                s.n1t[:, lo : lo + TILE] = jnp.transpose(s.n1[lo : lo + TILE, :])
 
         ex_kv.wait_recv()
-        for c in ex_r:
-            c.wait_recv()
+        ex_r.wait_recv()
 
         def unpack(packed):
             x = packed.astype(F32)
@@ -349,12 +349,15 @@
             use_exact = s.thr[h, 0:BLK, 0:BLK] < 2.5
             w_in = jnp.where(same_in, jnp.where(use_exact, exact, low_rank), 0.0).astype(BF16)
             s.win[h] = w_in
-            far0 = jnp.where(
-                s.mfar[0:BLK, :] > 0.5, nt(fq0, s.rin[h, 0]), 0.0
+            state = s.rin[h]
+            later = state.astype(F32) * s.link[0:1, :] + tn(
+                (v_in.astype(F32) * s.mprev[...]).astype(BF16), f_in
             )
+            s.rlater[h] = later.astype(BF16)
+            far0 = jnp.where(s.mfar[0:BLK, :] > 0.5, nt(fq0, state), 0.0)
             s.acc[h, 0:BLK, :] = s.acc[h, 0:BLK, :] + nn(w_in, v_in) + far0
             far1 = jnp.where(
-                s.mfar[BLK:T, :] > 0.5, nt(s.fq[h, BLK:T, :], s.rin[h, 1]), 0.0
+                s.mfar[BLK:T, :] > 0.5, nt(s.fq[h, BLK:T, :], s.rlater[h]), 0.0
             )
             s.acc[h, BLK:T, :] = s.acc[h, BLK:T, :] + far1
 
@@ -392,25 +395,31 @@
             c.wait_recv()
         c_wup.wait()
         c_wdown.wait()
-
-        def scatter_sum(make, bufs):
-            out, got = bufs.out, bufs.got
-            out[0] = make(h3).astype(BF16)
-            a = send(out.at[0], got.at[0], head=h1)
-            mine = make(h2)
+        if inner:
+            for j in range(nh):
+                lo = j * TILE
+                s.ogt[:, lo : lo + TILE] = jnp.transpose(s.og[j])
+
+        def scatter_beside(make, bufs):
+            bufs.out[0] = make(h3).astype(BF16)
+            a = send(bufs.out.at[0], bufs.got.at[0], head=h1)
+            bufs.mine[...] = make(h2)
+            return a
+
+        def scatter_across(bufs, a):
             a.wait_recv()
-            out[1] = (mine + got[0].astype(F32)).astype(BF16)
-            b = send(out.at[1], got.at[1], head=h2)
-            out[2] = make(h1).astype(BF16)
-            c = send(out.at[2], got.at[2], head=h1)
-            return (b, c)
-
-        def scatter_done(pending, bufs, own):
-            got = bufs.got
-            b, c = pending
+            bufs.out[1] = (bufs.mine[...] + bufs.got[0].astype(F32)).astype(BF16)
+            return send(bufs.out.at[1], bufs.got.at[1], head=h2)
+
+        def scatter_last(make, bufs):
+            bufs.out[2] = make(h1).astype(BF16)
+            return send(bufs.out.at[2], bufs.got.at[2], head=h1)
+
+        def scatter_done(bufs, b, c):
             c.wait_recv()
+            part = bufs.got[2].astype(F32)
             b.wait_recv()
-            return own + got[1].astype(F32) + got[2].astype(F32)
+            return part + bufs.got[1].astype(F32)
 
         def feed(slot):
             at = rows(slot)
@@ -427,51 +436,102 @@
             s.gu[at, :] = gu
             return nt(gu, s.wup[...])
 
-        pend = scatter_sum(feed, s.ra)
+        ra_a = scatter_beside(feed, s.ra)
+        ra_b = scatter_across(s.ra, ra_a)
+        ra_c = scatter_last(feed, s.ra)
         own = feed(head)
 
-        def weight_grad(name, left, right):
-            a = left(pl.ds(pl.multiple_of(other * half_rows, LANES), half_rows))
-            b = right()
-            if inner:
-                name.ys[...] = tn(a, b).astype(BF16)
-                c = send(name.ys, name.yr, seq=other)
-                a = left(pl.ds(pl.multiple_of(seq * half_rows, LANES), half_rows))
-                name.own[...] = tn(a, b)
-                return c
-            return None
-
-        def weight_cross(name, c):
-            c.wait_recv()
-            out = []
-            for d in range(1, nb):
-                at = rows(lax.rem(bat + d, nb), piece)
-                name.zs[d - 1] = (
-                    name.own[at, :] + name.yr[at, :].astype(F32)
-                ).astype(BF16)
-                out.append(
-                    send(
-                        name.zs.at[d - 1], name.zr.at[d - 1],
-                        batch=lax.rem(bat + d, nb),
-                    )
-                )
-            return out
-
-        def weight_sum(name, cs):
-            at = rows(bat, piece)
-            total = name.own[at, :] + name.yr[at, :].astype(F32)
-            for d, c in enumerate(cs):
-                c.wait_recv()
-                total = total + name.zr[d].astype(F32)
+        b1 = bat + 1 - 2 * lax.rem(bat, 2)
+        b2 = lax.rem(bat + 2, nb)
+        b3 = lax.rem(b1 + 2, nb)
+        there = pl.ds(pl.multiple_of(other * half_rows, LANES), half_rows)
+        here = pl.ds(pl.multiple_of(seq * half_rows, LANES), half_rows)
+
+        def y_send(g):
+            g.y = send(g.ys, g.yr, seq=other)
+
+        def y_other(g, left, right):
+            g.ys[...] = nn(left[there, :], right).astype(BF16)
+
+        def y_own(g, left, right):
+            g.own[...] = nn(left[here, :], right)
+
+        def with_y(g, index):
+            at = rows(index, piece)
+            return g.own[at, :] + g.yr[at, :].astype(F32)
+
+        def za_send(g):
+            g.y.wait_recv()
+            for i, index in enumerate((b1, b3)):
+                g.zas[i] = with_y(g, index).astype(BF16)
+            g.za = send(g.zas, g.zar, batch=b1)
+
+        def zb_send(g):
+            g.za.wait_recv()
+            g.zbs[...] = (with_y(g, b2) + g.zar[1].astype(F32)).astype(BF16)
+            g.zb = send(g.zbs, g.zbr, batch=b2)
+
+        def weight_sum(g):
+            total = with_y(g, bat) + g.zar[0].astype(F32)
+            g.zb.wait_recv()
+            return total + g.zbr[...].astype(F32)
+
+        def zd_send(g):
+            g.y.wait_recv()
+            g.zd = []
+            for i, index in enumerate((b2, b1, b3)):
+                g.zds[i] = with_y(g, index).astype(BF16)
+                g.zd.append(send(g.zds.at[i], g.zdr.at[i], batch=index))
+
+        def weight_sum_direct(g):
+            total = with_y(g, bat)
+            for i in (1, 2, 0):
+                g.zd[i].wait_recv()
+                total = total + g.zdr[i].astype(F32)
             return total
 
-        def og_cols(at):
-            return jnp.concatenate([s.og[j, :, at] for j in range(nh)], axis=0)
-
-        if inner:
-            y_down = weight_grad(s.wd, og_cols, lambda: s.act[...])
-
-        grad2 = scatter_done(pend, s.ra, own)
+        def both(index):
+            return [rows(half * nb + index, piece) for half in range(ns)]
+
+        def first_za(g, left, right):
+            g.own[...] = nn(left[...], right)
+            for i, index in enumerate((b1, b3)):
+                for half, at in enumerate(both(index)):
+                    g.zas[i, half] = g.own[at, :].astype(BF16)
+            g.za = send(g.zas, g.zar, batch=b1)
+
+        def first_zb(g):
+            g.za.wait_recv()
+            for half, at in enumerate(both(b2)):
+                g.zbs[half] = (g.own[at, :] + g.zar[1, half].astype(F32)).astype(BF16)
+            g.zb = send(g.zbs, g.zbr, batch=b2)
+
+        def first_part(g, half):
+            at = rows(half * nb + bat, piece)
+            return g.own[at, :] + g.zar[0, half].astype(F32) + g.zbr[half].astype(F32)
+
+        def first_y(g):
+            g.zb.wait_recv()
+            g.ys[...] = first_part(g, other).astype(BF16)
+            g.y = send(g.ys, g.yr, seq=other)
+
+        def first_sum(g):
+            total = first_part(g, seq)
+            g.y.wait_recv()
+            return total + g.yr[...].astype(F32)
+
+        def columns(ref, i, groups):
+            width = ref.shape[-1] // groups
+            return ref[:, i * width : (i + 1) * width]
+
+        if inner:
+            ups, qkvs = [s.u0, s.u1], [s.x0, s.x1, s.x2]
+            y_other(s.d1, s.ogt, columns(s.act, 1, 2))
+            y_send(s.d1)
+            first_za(s.d0, s.ogt, columns(s.act, 0, 2))
+            y_own(s.d1, s.ogt, columns(s.act, 1, 2))
+
+        grad2 = own + scatter_done(s.ra, ra_b, ra_c)
         mine = rows(head)
         xhat2, rstd2 = normalize(s.hid[mine, :])
         s.ns[...] = jnp.zeros_like(s.ns)
@@ -482,7 +542,18 @@
         s.gb[head] = grad_hidden.astype(BF16)
         ag_gb = gather_start(s.gb, 2)
         if inner:
-            y_up = weight_grad(s.wu, lambda at: s.n2[:, at], lambda: s.gu[...])
+            for j in range(nh):
+                lo = j * TILE
+                s.n2t[:, lo : lo + TILE] = jnp.transpose(s.n2[lo : lo + TILE, :])
+            y_other(s.u0, s.n2t, columns(s.gu, 0, 2))
+            y_send(s.u0)
+            y_other(s.u1, s.n2t, columns(s.gu, 1, 2))
+
+        def lower(slot):
+            return nn(s.act[rows(slot), :], s.wdown[...])
+
+        rc_a = scatter_beside(lower, s.rc)
+        rc_c = scatter_last(lower, s.rc)
 
         def divide_back(slot):
             at = rows(slot)
@@ -500,6 +571,9 @@
         for _, c, _, _ in ag_gb:
             c.wait_recv()
         divide_back(h1)
+        if inner:
+            first_zb(s.d0)
+            za_send(s.d1)
         fw_gb = gather_forward(s.gb, ag_gb)
         divide_back(h2)
         for c in fw_gb:
@@ -513,8 +587,11 @@
         for h in range(H):
             gm = jnp.where(s.mfar[...] > 0.5, s.gn[h].astype(F32), 0.0).astype(BF16)
             s.gm[h] = gm
-            s.grout[h, 0] = tn(gm[0:BLK, :], s.fq[h, 0:BLK, :])[:STATE].astype(BF16)
-            s.grout[h, 1] = tn(gm[BLK:T, :], s.fq[h, BLK:T, :])[:STATE].astype(BF16)
+            glater = tn(gm[BLK:T, :], s.fq[h, BLK:T, :])
+            gstate = tn(gm[0:BLK, :], s.fq[h, 0:BLK, :]) + glater * s.link[0:1, :]
+            s.grout[h] = gstate[:STATE].astype(BF16)
+            glater = glater.astype(BF16)
+            v_last = (s.vin[h].astype(F32) * s.mprev[...]).astype(BF16)
             gn0 = s.gn[h, 0:BLK, :]
             q0 = s.q[h, 0:BLK, :]
             fq0 = s.fq[h, 0:BLK, :]
@@ -525,20 +602,22 @@
                 same_in & use_exact, gw * w_in.astype(F32) * (1.0 / math.sqrt(DH)), 0.0
             ).astype(BF16)
             gp = jnp.where(same_in & jnp.logical_not(use_exact), gw, 0.0).astype(BF16)
-            gk = feature_back(tn(gp, fq0), s.fin[h], s.kin[h]) + tn(gs, q0)
-            gv = tn(w_in, gn0)
+            gfeat = tn(gp, fq0) + nn(v_last, glater)
+            gk = feature_back(gfeat, s.fin[h], s.kin[h]) + tn(gs, q0)
+            gv = tn(w_in, gn0) + s.mprev[...] * nt(s.fin[h], glater)
             s.gkvout[h] = jnp.where(low, gk, pltpu.roll(gv, DH, 1)).astype(BF16)
             s.gfq0[h] = nn(gp, s.fin[h])
             s.gq0[h] = nn(gs, s.kin[h])
         ex_gkv = send(s.gkvout, s.gkvin, seq=other)
-        ex_gr = [
-            send(s.grout.at[h], s.grin.at[h, :, pl.ds(0, STATE)], seq=other) for h in range(H)
-        ]
-
-        if inner:
-            z_down = weight_cross(s.wd, y_down)
-
-        def attend_back(h, carry):
+        ex_gr = send(s.grout, s.grin.at[:, pl.ds(0, STATE)], seq=other)
+
+        rc_b = scatter_across(s.rc, rc_a)
+        if inner:
+            y_send(s.u1)
+            for i, g in enumerate(ups):
+                y_own(g, s.n2t, columns(s.gu, i, 2))
+
+        def attend_back(h):
             for t in range(nt_tiles):
                 lo, hi = t * TILE, (t + 1) * TILE
                 w0 = max(0, lo - TILE)
@@ -565,14 +644,14 @@
                 gq = nn(gs, s.k[h, w0:hi, :])
                 gm = s.gm[h, lo:hi, :]
                 if t == 0:
-                    top = nn(gm[0:BLK], s.rin[h, 0]) + s.gfq0[h]
-                    bottom = nn(gm[BLK:], s.rin[h, 1])
+                    top = nn(gm[0:BLK], s.rin[h]) + s.gfq0[h]
+                    bottom = nn(gm[BLK:], s.rlater[h])
                     gfq = gfq + jnp.concatenate([top, bottom], axis=0)
                     gq = gq + jnp.concatenate(
                         [s.gq0[h], jnp.zeros((TILE - BLK, LANES), F32)], axis=0
                     )
                 else:
-                    gfq = gfq + nn(gm, s.rin[h, 1])
+                    gfq = gfq + nn(gm, s.rlater[h])
                 gq = gq + feature_back(gfq, s.fq[h, lo:hi, :], s.q[h, lo:hi, :])
                 s.gq[h, lo:hi, :] = gq
             for t in range(nt_tiles):
@@ -583,28 +662,28 @@
                 if t + 1 < nt_tiles:
                     gk = gk + tn(s.gs[hi : hi + TILE, :TILE], s.q[h, hi : hi + TILE, :])
                 s.gk[h, lo:hi, :] = gk
-            return carry
-
-        lax.fori_loop(0, H, attend_back, 0)
-
-        def gb_cols(at):
-            return jnp.concatenate([s.gb[j, :, at] for j in range(nh)], axis=0)
-
-        if inner:
-            y_out = weight_grad(s.wo_g, gb_cols, lambda: s.at[head])
-            z_up = weight_cross(s.wu, y_up)
+
+        for h in range(H):
+            attend_back(h)
+            if inner and h == 1:
+                za_send(s.u0)
+        if inner:
+            zb_send(s.d1)
+            first_y(s.d0)
+            for j in range(nh):
+                lo = j * TILE
+                s.gbt[:, lo : lo + TILE] = jnp.transpose(s.gb[j])
+            y_other(s.o0, s.gbt, s.at[head])
+            y_send(s.o0)
 
         ex_gkv.wait_recv()
-        for c in ex_gr:
-            c.wait_recv()
+        ex_gr.wait_recv()
 
         def finish(h, carry):
-            v1, v0 = s.v1[h], s.v0[h]
-            r0 = jnp.where(first, s.grin[h, 0].astype(F32), 0.0).astype(BF16)
-            r1 = jnp.where(first, s.grin[h, 1].astype(F32), 0.0).astype(BF16)
-            gfk = s.gfk[h] + nn(v0, r0) + nn(v1, r1)
+            state = jnp.where(first, s.grin[h].astype(F32), 0.0).astype(BF16)
+            gfk = s.gfk[h] + nn(s.v0[h], state)
             fk = s.fk[h]
-            gv = s.gv[h] + s.m0[...] * nt(fk, r0) + s.m1[...] * nt(fk, r1)
+            gv = s.gv[h] + s.m0[...] * nt(fk, state)
             gk = s.gk[h] + feature_back(gfk, fk, s.k[h])
             s.gk[h] = gk
             s.gv[h] = gv
@@ -626,48 +705,64 @@
                 s.gqkv[:, i * DH : (i + 1) * DH] = a[:, :DH].astype(BF16)
 
         if inner:
-            y_qkv = weight_grad(s.wx, lambda at: s.n1[:, at], lambda: s.gqkv[...])
-
-        pend = scatter_sum(lambda slot: nn(s.gqkv[rows(slot), :], s.wqkv[...]), s.rb)
-        own = nn(s.gqkv[mine, :], s.wqkv[...])
-        if inner:
-            z_out = weight_cross(s.wo_g, y_out)
-
-        pend_mixed = scatter_sum(lambda slot: nn(s.act[rows(slot), :], s.wdown[...]), s.rc)
-        own_mixed = nn(s.act[mine, :], s.wdown[...])
-
-        grad1 = scatter_done(pend, s.rb, own)
+            for i, g in enumerate(qkvs):
+                y_other(g, s.n1t, columns(s.gqkv, i, 3))
+                y_send(g)
+
+        def first_grad(slot):
+            return nn(s.gqkv[rows(slot), :], s.wqkv[...])
+
+        rb_a = scatter_beside(first_grad, s.rb)
+        rb_b = scatter_across(s.rb, rb_a)
+        if inner:
+            zb_send(s.u0)
+        rb_c = scatter_last(first_grad, s.rb)
+        own = first_grad(head)
+        if inner:
+            za_send(s.u1)
+            y_own(s.o0, s.gbt, s.at[head])
+            for i, g in enumerate(qkvs):
+                y_own(g, s.n1t, columns(s.gqkv, i, 3))
+            zd_send(s.o0)
+        own_mixed = s.hid[mine, :] + lower(head)
+
+        grad1 = own + scatter_done(s.rb, rb_b, rb_c)
         xhat1, rstd1 = normalize(s.tok[head].astype(F32))
         s.ns[0:1, :] = jnp.sum(grad1 * xhat1, axis=0, keepdims=True)
         s.ns[1:2, :] = jnp.sum(grad1, axis=0, keepdims=True)
         gtok_ref[0] = s.gh[...] + norm_back(grad1, gain1, xhat1, rstd1)
 
         if inner:
-            n_z = [
-                send(s.ns, s.nz.at[d - 1], batch=lax.rem(bat + d, nb)) for d in range(1, nb)
-            ]
-            z_qkv = weight_cross(s.wx, y_qkv)
-        mixed_ref[0] = (s.hid[mine, :] + scatter_done(pend_mixed, s.rc, own_mixed)).astype(BF16)
-
-        if inner:
+            n_h = [send(s.ns, s.nh.at[i], head=d) for i, d in enumerate((h1, h2, h3))]
+            zd_send(s.x0)
+            zb_send(s.u1)
             total = s.ns[...]
-            for d, c in enumerate(n_z):
-                c.wait_recv()
-                total = total + s.nz[d]
-            s.ns2[...] = total
-            c = send(s.ns2, s.ny, seq=other)
-            odown_ref[...] = weight_sum(s.wd, z_down)
-            oup_ref[...] = weight_sum(s.wu, z_up)
-            c.wait_recv()
-            s.ns3[...] = total + s.ny[...]
-            n_h = [send(s.ns3, s.nh.at[i], head=d) for i, d in enumerate((h1, h2, h3))]
-            s.otmp[...] = jnp.zeros_like(s.otmp)
-            s.otmp[0:piece, 0:E] = weight_sum(s.wo_g, z_out)
-            oout_ref[...] = jnp.transpose(s.otmp[...])[:E, :piece]
-            total = s.ns3[...]
             for i, c in enumerate(n_h):
                 c.wait_recv()
                 total = total + s.nh[i]
+            s.ns2[...] = total
+            n_y = send(s.ns2, s.ny, seq=other)
+            zd_send(s.x1)
+        mixed_ref[0] = (own_mixed + scatter_done(s.rc, rc_b, rc_c)).astype(BF16)
+        if inner:
+            n_y.wait_recv()
+            s.ns3[...] = s.ns2[...] + s.ny[...]
+            n_z = [
+                send(s.ns3, s.nz.at[d - 1], batch=lax.rem(bat + d, nb)) for d in range(1, nb)
+            ]
+            zd_send(s.x2)
+            wide = FL // 2
+            odown_ref[:, :wide] = first_sum(s.d0)
+            odown_ref[:, wide:] = weight_sum(s.d1)
+            oup_ref[:, :wide] = weight_sum(s.u0)
+            oup_ref[:, wide:] = weight_sum(s.u1)
+            s.otmp[...] = jnp.zeros_like(s.otmp)
+            s.otmp[0:piece, 0:E] = weight_sum_direct(s.o0)
+            oout_ref[...] = jnp.transpose(s.otmp[...])[:E, :piece]
+            total = s.ns3[...]
+            for i, c in enumerate(n_z):
+                c.wait_recv()
+                total = total + s.nz[i]
             width = D // (ns * nb * nh)
             start = ((seq * nb + bat) * nh + head) * width
             pick = (
@@ -678,14 +773,17 @@
                 total, pick, (((1,), (0,)), ((), ())),
                 precision=lax.Precision.HIGHEST, preferred_element_type=F32,
             )
-            gx = weight_sum(s.wx, z_qkv)
-            for c in range(3):
-                oqkv_ref[c] = gx[:, c * E : (c + 1) * E]
+            for i, g in enumerate(qkvs):
+                oqkv_ref[i] = weight_sum_direct(g)
         else:
+
+            def joined(ref):
+                return jnp.concatenate([ref[j] for j in range(nh)], axis=0)
+
             norm_ref[...] = s.ns[...]
-            odown_ref[...] = tn(og_cols(slice(0, D)), s.act[...])
+            odown_ref[...] = tn(joined(s.og), s.act[...])
             oup_ref[...] = tn(s.n2[...], s.gu[...])
-            oout_ref[...] = tn(gb_cols(slice(0, D)), s.at[head])
+            oout_ref[...] = tn(joined(s.gb), s.at[head])
             oqkv_ref[...] = tn(s.n1[...], s.gqkv[...])
         for c in sends:
             c.wait_send()
@@ -710,7 +808,8 @@
         segrow=((8, T), F32),
         segcol=((T, LANES), F32),
         m0=((T, LANES), F32),
-        m1=((T, LANES), F32),
+        mprev=((BLK, LANES), F32),
+        link=((8, M), F32),
         mfar=((T, LANES), F32),
         thr=((H, T, LANES), F32),
         code=((T // TILE, TILE, 2 * TILE), F32),
@@ -722,15 +821,15 @@
         k=((H, T, LANES), BF16),
         v=((H, T, LANES), BF16),
         v0=((H, T, LANES), BF16),
-        v1=((H, T, LANES), BF16),
         gn=((H, T, LANES), BF16),
         gm=((H, T, LANES), BF16),
         fq=((H, T, M), BF16),
         fk=((H, T, M), BF16),
-        rout=((H, 2, STATE, M), BF16),
-        grout=((H, 2, STATE, M), BF16),
-        rin=((H, 2, LANES, M), BF16),
-        grin=((H, 2, LANES, M), BF16),
+        rout=((H, STATE, M), BF16),
+        grout=((H, STATE, M), BF16),
+        rin=((H, LANES, M), BF16),
+        grin=((H, LANES, M), BF16),
+        rlater=((H, LANES, M), BF16),
         kvout=((H, BLK, LANES), BF16),
         kvin=((H, BLK, LANES), BF16),
         gkvout=((H, BLK, LANES), BF16),
@@ -759,7 +858,7 @@
         gqkv=((T, 3 * E), BF16),
         ns=((8, D), F32),
     )
-    pair = dict(out=((3, R, D), BF16), got=((3, R, D), BF16))
+    pair = dict(out=((3, R, D), BF16), got=((3, R, D), BF16), mine=((R, D), F32))
     plan.group(ra=pair, rb=pair, rc=pair)
     if inner:
 
@@ -768,11 +867,38 @@
                 ys=((half, width), BF16),
                 yr=((half, width), BF16),
                 own=((half, width), F32),
-                zs=((nb - 1, piece, width), BF16),
-                zr=((nb - 1, piece, width), BF16),
+                zas=((2, piece, width), BF16),
+                zar=((2, piece, width), BF16),
+                zbs=((piece, width), BF16),
+                zbr=((piece, width), BF16),
             )
 
-        plan.group(wd=weight(FL), wu=weight(FL), wo_g=weight(E), wx=weight(3 * E))
+        def weight_direct(width):
+            return dict(
+                ys=((half, width), BF16),
+                yr=((half, width), BF16),
+                own=((half, width), F32),
+                zds=((nb - 1, piece, width), BF16),
+                zdr=((nb - 1, piece, width), BF16),
+            )
+
+        def weight_first(width):
+            return dict(
+                own=((D, width), F32),
+                zas=((2, ns, piece, width), BF16),
+                zar=((2, ns, piece, width), BF16),
+                zbs=((ns, piece, width), BF16),
+                zbr=((ns, piece, width), BF16),
+                ys=((piece, width), BF16),
+                yr=((piece, width), BF16),
+            )
+
+        wide = weight(FL // 2)
+        plan.group(d0=weight_first(FL // 2), d1=wide, u0=wide, u1=wide)
+        narrow = weight_direct(E)
+        plan.group(o0=narrow, x0=narrow, x1=narrow, x2=narrow)
+        turned = ((D, T), BF16)
+        plan.add(n1t=turned, n2t=turned, ogt=turned, gbt=turned)
         plan.add(
             ns2=((8, D), F32),
             ns3=((8, D), F32),
@@ -790,7 +916,7 @@
         grads = [(D, 3 * E), (D, E), (D, FL), (D, FL)]
         norm = (8, D)
     outs = [((1, R, D), BF16), ((1, R, D), F32), (norm, F32)] + [(g, F32) for g in grads]
-    hbm = pl.BlockSpec(memory_space=pl.ANY)
+    hbm = pl.BlockSpec(memory_space=pltpu.HBM)
     vmem = pl.BlockSpec(memory_space=pltpu.VMEM)
     in_specs = [hbm, vmem, vmem, vmem, vmem, vmem, hbm, hbm, vmem, vmem, hbm, hbm, hbm]
     kernel = make_kernel(dims, len(in_specs), len(outs), plan)
@@ -805,6 +931,28 @@
         ),
         name="block",
     )
+
+
+def hand_over(width, *arrays):
+    count = len(arrays) - 1
+
+    def kernel(*refs):
+        ins, norm_ref = refs[:count], refs[count]
+        outs, norm_outs = refs[count + 1 : 2 * count + 1], refs[2 * count + 1 :]
+        for a, b in zip(ins, outs):
+            b[...] = a[...]
+        for i, out in enumerate(norm_outs):
+            out[...] = norm_ref[i, :width]
+
+    vmem = pl.BlockSpec(memory_space=pltpu.VMEM)
+    return pl.pallas_call(
+        kernel,
+        out_shape=[jax.ShapeDtypeStruct(a.shape, a.dtype) for a in arrays[:-1]]
+        + [jax.ShapeDtypeStruct((width,), F32)] * 4,
+        in_specs=[vmem] * len(arrays),
+        out_specs=[vmem] * (count + 4),
+        name="hand_over",
+    )(*arrays)
 
 
 def per_device(
@@ -829,17 +977,18 @@
     E = w_qkv.shape[2]
     FL = w_up.shape[1]
     piece = D // (ns * nb)
-    inner = piece % 16 == 0
+    inner = piece % 16 == 0 and nb == 4
     dims = (nh, ns, nb, T, rows, D, E, FL, E // DH, omega.shape[1], inner)
     w_flat = jnp.transpose(w_qkv, (1, 2, 0)).reshape(3 * E, D)
-    row = lambda a: a.reshape(1, D)
     mixed, grad_tokens, norms, g_qkv, g_out, g_up, g_down = build(dims)(
-        tokens, seg_ids, pattern, omega, row(norm1_gain), row(norm1_bias), w_flat, w_out,
-        row(norm2_gain), row(norm2_bias), w_up, w_down, out_grad,
+        tokens, seg_ids, pattern, omega, norm1_gain, norm1_bias, w_flat, w_out,
+        norm2_gain, norm2_bias, w_up, w_down, out_grad,
     )
     if inner:
         width = D // (ns * nb * nh)
-        norms = norms[:, :width]
+        mixed, grad_tokens, g_qkv, g_out, g_up, g_down, *norms = hand_over(
+            width, mixed, grad_tokens, g_qkv, g_out, g_up, g_down, norms
+        )
         g_qkv = jnp.transpose(g_qkv, (1, 0, 2))
         g_down = g_down.T
     else:

time: 115 us -> 99.1 us (0.86)
  local copies, waits for them, and re-layouts: 12.7 us -> 0 us
  Pallas kernels: 102 us -> 98.1 us
    unnamed x14 -> x0, local copies, waits for them, and re-layouts: 6.22 us -> none
    pallas_call x1, Pallas kernels: 102 us -> 95.6 us  [per_device(): build(dims)]
    reshape x4 -> x0, local copies, waits for them, and re-layouts: 5.07 us -> none  [per_device(): row = lambda a: a.reshape(1, D)]
    pallas_call x0 -> x1, Pallas kernels: none -> 2.54 us  [hand_over(): pl.pallas_call(kernel, out_shape=[jax.ShapeDtypeStruct(a.shape, a.dtype)...]
    squeeze x1 -> x0, local copies, waits for them, and re-layouts: 1.36 us -> none  [per_device(): norms[3]]
where the time goes in v2:
time: 99.1 us; the launch traced here: 98.9 us
  Pallas kernels  98.1 us (99%)
    pallas_call x1, Pallas kernels, per_device(): build(dims)  95.6 us
    pallas_call x1, Pallas kernels, hand_over(): pl.pallas_call(kernel, out_shape=[jax.ShapeDtypeStruct(a.shape, a.dtype)...  2.54 us

profile of v2, /device:TPU:0, one launch (start us, length us, event | category | flops | bytes accessed | tf_op | source)
XLA Modules:
  0.0 98.9 jit_solution(2797740394116130278)
XLA Ops:
  0.6 95.6 %block.1 = (bf16[1,128,768]{2,1,0:T(8,128)(2,1)}, f32[1,128,768]{2,1,0:T(8,128)}, f32[8,128]{1,0:T(8,128)}, f32[3,96,192]{2,1,0:T(8,128)}, f32[192,96]{1,0:T(8,1...) custom-call(bf16[1,128,768]{2,1,0:T(8,128)(2,1)} %refs_0_.1, s32[1,1024]{1,0:T(1,128)} %refs_1_.1, s32[3,16]{1,0:T(4,128)} %refs_2_.1, ...), custom_call_target="tpu_custom_call" | custom-call | tf_op jit(solution)/shard_map/block/pallas_call | solution.py:983
  96.2 2.5 %hand_over.1 = (bf16[1,128,768]{2,1,0:T(8,128)(2,1)}, f32[1,128,768]{2,1,0:T(8,128)}, f32[3,96,192]{2,1,0:T(8,128)}, f32[192,96]{1,0:T(8,128)}, f32[96,768]{1,0:...) custom-call(bf16[1,128,768]{2,1,0:T(8,128)(2,1)} %get-tuple-element.27.refs_0_, ...), custom_call_target="tpu_custom_call" | custom-call | tf_op jit(solution)/shard_map/hand_over/pallas_call | solution.py:948

commit v3 on v2

--- a/solution.py
+++ b/solution.py
@@ -127,6 +127,14 @@
             c.start()
             sends.append(c)
             return c
+
+        def prepare(src, dst, **dev):
+            k = used["r"]
+            used["r"] += 1
+            return pltpu.make_async_remote_copy(
+                src_ref=src, dst_ref=dst, send_sem=ssem.at[k], recv_sem=rsem.at[k],
+                device_id=dev, device_id_type=MESH,
+            )
 
         def rows(slot, n=TILE):
             return pl.ds(pl.multiple_of(slot * n, n), n)
@@ -366,9 +374,9 @@
             inv = 1.0 / acc[:, DH : DH + 1]
             return acc * inv, inv
 
-        ag_at = []
-        fw_at = []
-        for t in range(nt_tiles):
+        order = (0, 2, 1, 3)
+        ag_at = {}
+        for t in order:
             lo, hi = t * TILE, (t + 1) * TILE
             outs = [divided(h, lo, hi)[0] for h in range(H)]
             for h in range(0, H, 2):
@@ -378,20 +386,15 @@
                 else:
                     s.at[head, lo:hi, h * DH : (h + 1) * DH] = outs[h][:, :DH].astype(BF16)
             part = s.at.at[head, pl.ds(lo, TILE)]
-            ag_at.append((send(part, part, head=h2), send(part, part, head=h1), lo, TILE))
+            ag_at[t] = (send(part, part, head=h2), send(part, part, head=h1))
         for c in fw_wo:
             c.wait_recv()
         for _, c, _, _ in ag_wo:
             c.wait_recv()
-        fw_at = gather_forward(s.at, ag_at)
         fw_og = gather_forward(s.og, ag_og)
         for _, c, _, _ in ag_og:
             c.wait_recv()
         for c in fw_og:
-            c.wait_recv()
-        for _, c, _, _ in ag_at:
-            c.wait_recv()
-        for c in fw_at:
             c.wait_recv()
         c_wup.wait()
         c_wdown.wait()
@@ -399,6 +402,12 @@
             for j in range(nh):
                 lo = j * TILE
                 s.ogt[:, lo : lo + TILE] = jnp.transpose(s.og[j])
+        fw_at = {}
+
+        def forward_attended(t):
+            ag_at[t][0].wait_recv()
+            part = s.at.at[h2, pl.ds(t * TILE, TILE)]
+            fw_at[t] = send(part, part, head=h1)
 
         def scatter_beside(make, bufs):
             bufs.out[0] = make(h3).astype(BF16)
@@ -422,7 +431,9 @@
             return part + bufs.got[1].astype(F32)
 
         def feed(slot):
-            at = rows(slot)
+            ag_at[slot][1].wait_recv()
+            fw_at[slot].wait_recv()
+            at = slice(slot * TILE, (slot + 1) * TILE)
             hid = s.tok[slot].astype(F32)
             for j in range(nh):
                 hid = hid + nn(s.at[j, at, :], s.wo[j])
@@ -434,12 +445,36 @@
             s.act[at, :] = act.astype(BF16)
             gu = (nt(s.og[slot], s.wdown[...]) * slope).astype(BF16)
             s.gu[at, :] = gu
-            return nt(gu, s.wup[...])
-
-        ra_a = scatter_beside(feed, s.ra)
-        ra_b = scatter_across(s.ra, ra_a)
-        ra_c = scatter_last(feed, s.ra)
-        own = feed(head)
+            s.ra.part[slot] = nt(gu, s.wup[...])
+
+        core = lax.rem(head, 2)
+        ra_a = {
+            t: prepare(s.ra.out.at[t], s.ra.got.at[t], head=h1) for t in range(nh)
+        }
+        ra_b = prepare(s.ra.bout, s.ra.bgot, head=h2)
+
+        def to_core(t):
+            @pl.when(core != t % 2)
+            def _():
+                s.ra.out[t] = s.ra.part[t].astype(BF16)
+                ra_a[t].start()
+
+        def to_chip(t):
+            @pl.when(h2 == t)
+            def _():
+                ra_a[t].wait_recv()
+                s.ra.bout[...] = (s.ra.part[t] + s.ra.got[t].astype(F32)).astype(BF16)
+                ra_b.start()
+
+        forward_attended(order[0])
+        for i, t in enumerate(order):
+            if i + 1 < nh:
+                forward_attended(order[i + 1])
+            feed(t)
+            to_core(t)
+            if i > 0:
+                to_chip(order[i - 1])
+        to_chip(order[-1])
 
         b1 = bat + 1 - 2 * lax.rem(bat, 2)
         b2 = lax.rem(bat + 2, nb)
@@ -448,13 +483,10 @@
         here = pl.ds(pl.multiple_of(seq * half_rows, LANES), half_rows)
 
         def y_send(g):
+            right = g.right()
+            g.ys[...] = nn(g.left[there, :], right).astype(BF16)
             g.y = send(g.ys, g.yr, seq=other)
-
-        def y_other(g, left, right):
-            g.ys[...] = nn(left[there, :], right).astype(BF16)
-
-        def y_own(g, left, right):
-            g.own[...] = nn(left[here, :], right)
+            g.own[...] = nn(g.left[here, :], right)
 
         def with_y(g, index):
             at = rows(index, piece)
@@ -493,8 +525,8 @@
         def both(index):
             return [rows(half * nb + index, piece) for half in range(ns)]
 
-        def first_za(g, left, right):
-            g.own[...] = nn(left[...], right)
+        def first_za(g):
+            g.own[...] = nn(g.left[...], g.right())
             for i, index in enumerate((b1, b3)):
                 for half, at in enumerate(both(index)):
                     g.zas[i, half] = g.own[at, :].astype(BF16)
@@ -520,18 +552,61 @@
             g.y.wait_recv()
             return total + g.yr[...].astype(F32)
 
-        def columns(ref, i, groups):
-            width = ref.shape[-1] // groups
-            return ref[:, i * width : (i + 1) * width]
-
+        def collect(g):
+            if hasattr(g, "zdr"):
+                return weight_sum_direct(g)
+            return weight_sum(g) if g.zbs.shape[0] == piece else first_sum(g)
+
+        def chunks(groups, left, ref):
+            width = ref.shape[-1] // len(groups)
+            for i, g in enumerate(groups):
+                g.left = left
+                g.right = lambda i=i: ref[:, i * width : (i + 1) * width]
+
+        steps = {}
         if inner:
-            ups, qkvs = [s.u0, s.u1], [s.x0, s.x1, s.x2]
-            y_other(s.d1, s.ogt, columns(s.act, 1, 2))
-            y_send(s.d1)
-            first_za(s.d0, s.ogt, columns(s.act, 0, 2))
-            y_own(s.d1, s.ogt, columns(s.act, 1, 2))
-
-        grad2 = own + scatter_done(s.ra, ra_b, ra_c)
+            downs, ups, qkvs = (s.d0, s.d1), (s.u0, s.u1), (s.x0, s.x1, s.x2)
+            chunks(downs, s.ogt, s.act)
+            chunks(ups, s.n2t, s.gu)
+            chunks((s.o0,), s.gbt, s.at.at[head])
+            chunks(qkvs, s.n1t, s.gqkv)
+            steps = {
+                0: [(first_za, s.d1)],
+                1: [(y_send, s.d0)],
+                5: [(y_send, s.u0)],
+                6: [(first_za, s.u1)],
+                7: [(first_zb, s.d1)],
+                9: [(za_send, s.d0)],
+                15: [(first_zb, s.u1)],
+                17: [(y_send, s.o0)],
+                19: [(za_send, s.u0)],
+                21: [(y_send, s.x0)],
+                24: [(zb_send, s.d0)],
+                27: [(za_send, s.o0), (y_send, s.x1)],
+                28: [(zb_send, s.u0), (za_send, s.x0)],
+                29: [(y_send, s.x2), (zb_send, s.o0), (zd_send, s.x1)],
+                30: [(first_y, s.d1)],
+                31: [(za_send, s.x2)],
+                34: [(zb_send, s.x0)],
+                36: [(first_y, s.u1)],
+                37: [(zb_send, s.x2)],
+            }
+
+        def run(*numbers):
+            for number in numbers:
+                for step, group in steps.get(number, ()):
+                    step(group)
+
+        run(0, 1)
+        for t in range(nh):
+
+            @pl.when(head == t)
+            def _():
+                ra_a[t].wait_recv()
+
+        ra_b.wait_recv()
+        run(2)
+        grad2 = s.ra.part[head] + s.ra.got[head].astype(F32) + s.ra.bgot[...].astype(F32)
         mine = rows(head)
         xhat2, rstd2 = normalize(s.hid[mine, :])
         s.ns[...] = jnp.zeros_like(s.ns)
@@ -540,20 +615,21 @@
         grad_hidden = s.og[head].astype(F32) + norm_back(grad2, gain2, xhat2, rstd2)
         s.gh[...] = grad_hidden
         s.gb[head] = grad_hidden.astype(BF16)
+        run(3)
         ag_gb = gather_start(s.gb, 2)
+        run(4)
         if inner:
             for j in range(nh):
                 lo = j * TILE
                 s.n2t[:, lo : lo + TILE] = jnp.transpose(s.n2[lo : lo + TILE, :])
-            y_other(s.u0, s.n2t, columns(s.gu, 0, 2))
-            y_send(s.u0)
-            y_other(s.u1, s.n2t, columns(s.gu, 1, 2))
+        run(5, 6)
 
         def lower(slot):
             return nn(s.act[rows(slot), :], s.wdown[...])
 
         rc_a = scatter_beside(lower, s.rc)
         rc_c = scatter_last(lower, s.rc)
+        run(7)
 
         def divide_back(slot):
             at = rows(slot)
@@ -571,14 +647,14 @@
         for _, c, _, _ in ag_gb:
             c.wait_recv()
         divide_back(h1)
-        if inner:
-            first_zb(s.d0)
-            za_send(s.d1)
+        run(8)
         fw_gb = gather_forward(s.gb, ag_gb)
         divide_back(h2)
         for c in fw_gb:
             c.wait_recv()
+        run(9)
         divide_back(h3)
+        run(10)
 
         def feature_back(gfeat, feat, twice):
             x = nn((gfeat * feat.astype(F32)).astype(BF16), s.omt[...])
@@ -608,14 +684,13 @@
             s.gkvout[h] = jnp.where(low, gk, pltpu.roll(gv, DH, 1)).astype(BF16)
             s.gfq0[h] = nn(gp, s.fin[h])
             s.gq0[h] = nn(gs, s.kin[h])
+        run(11)
         ex_gkv = send(s.gkvout, s.gkvin, seq=other)
         ex_gr = send(s.grout, s.grin.at[:, pl.ds(0, STATE)], seq=other)
 
+        run(12)
         rc_b = scatter_across(s.rc, rc_a)
-        if inner:
-            y_send(s.u1)
-            for i, g in enumerate(ups):
-                y_own(g, s.n2t, columns(s.gu, i, 2))
+        run(13)
 
         def attend_back(h):
             for t in range(nt_tiles):
@@ -665,19 +740,16 @@
 
         for h in range(H):
             attend_back(h)
-            if inner and h == 1:
-                za_send(s.u0)
+            run(14 + min(h, 2))
         if inner:
-            zb_send(s.d1)
-            first_y(s.d0)
             for j in range(nh):
                 lo = j * TILE
                 s.gbt[:, lo : lo + TILE] = jnp.transpose(s.gb[j])
-            y_other(s.o0, s.gbt, s.at[head])
-            y_send(s.o0)
+        run(17)
 
         ex_gkv.wait_recv()
         ex_gr.wait_recv()
+        run(18)
 
         def finish(h, carry):
             state = jnp.where(first, s.grin[h].astype(F32), 0.0).astype(BF16)
@@ -704,60 +776,57 @@
             else:
                 s.gqkv[:, i * DH : (i + 1) * DH] = a[:, :DH].astype(BF16)
 
-        if inner:
-            for i, g in enumerate(qkvs):
-                y_other(g, s.n1t, columns(s.gqkv, i, 3))
-                y_send(g)
+        run(19, 20, 21, 22)
 
         def first_grad(slot):
             return nn(s.gqkv[rows(slot), :], s.wqkv[...])
 
         rb_a = scatter_beside(first_grad, s.rb)
+        run(23)
         rb_b = scatter_across(s.rb, rb_a)
-        if inner:
-            zb_send(s.u0)
+        run(24)
         rb_c = scatter_last(first_grad, s.rb)
+        run(25)
         own = first_grad(head)
-        if inner:
-            za_send(s.u1)
-            y_own(s.o0, s.gbt, s.at[head])
-            for i, g in enumerate(qkvs):
-                y_own(g, s.n1t, columns(s.gqkv, i, 3))
-            zd_send(s.o0)
+        run(26)
         own_mixed = s.hid[mine, :] + lower(head)
 
+        run(27, 28)
         grad1 = own + scatter_done(s.rb, rb_b, rb_c)
+        run(29)
         xhat1, rstd1 = normalize(s.tok[head].astype(F32))
         s.ns[0:1, :] = jnp.sum(grad1 * xhat1, axis=0, keepdims=True)
         s.ns[1:2, :] = jnp.sum(grad1, axis=0, keepdims=True)
         gtok_ref[0] = s.gh[...] + norm_back(grad1, gain1, xhat1, rstd1)
 
         if inner:
+            run(30)
             n_h = [send(s.ns, s.nh.at[i], head=d) for i, d in enumerate((h1, h2, h3))]
-            zd_send(s.x0)
-            zb_send(s.u1)
+            run(31)
             total = s.ns[...]
             for i, c in enumerate(n_h):
                 c.wait_recv()
                 total = total + s.nh[i]
             s.ns2[...] = total
+            run(32)
             n_y = send(s.ns2, s.ny, seq=other)
-            zd_send(s.x1)
+            run(33)
         mixed_ref[0] = (own_mixed + scatter_done(s.rc, rc_b, rc_c)).astype(BF16)
         if inner:
+            run(34)
             n_y.wait_recv()
+            run(35)
             s.ns3[...] = s.ns2[...] + s.ny[...]
             n_z = [
                 send(s.ns3, s.nz.at[d - 1], batch=lax.rem(bat + d, nb)) for d in range(1, nb)
             ]
-            zd_send(s.x2)
+            run(36, 37)
             wide = FL // 2
-            odown_ref[:, :wide] = first_sum(s.d0)
-            odown_ref[:, wide:] = weight_sum(s.d1)
-            oup_ref[:, :wide] = weight_sum(s.u0)
-            oup_ref[:, wide:] = weight_sum(s.u1)
+            for i in range(2):
+                odown_ref[:, i * wide : (i + 1) * wide] = collect(downs[i])
+                oup_ref[:, i * wide : (i + 1) * wide] = collect(ups[i])
             s.otmp[...] = jnp.zeros_like(s.otmp)
-            s.otmp[0:piece, 0:E] = weight_sum_direct(s.o0)
+            s.otmp[0:piece, 0:E] = collect(s.o0)
             oout_ref[...] = jnp.transpose(s.otmp[...])[:E, :piece]
             total = s.ns3[...]
             for i, c in enumerate(n_z):
@@ -774,7 +843,7 @@
                 precision=lax.Precision.HIGHEST, preferred_element_type=F32,
             )
             for i, g in enumerate(qkvs):
-                oqkv_ref[i] = weight_sum_direct(g)
+                oqkv_ref[i] = collect(g)
         else:
 
             def joined(ref):
@@ -785,6 +854,13 @@
             oup_ref[...] = tn(s.n2[...], s.gu[...])
             oout_ref[...] = tn(joined(s.gb), s.at[head])
             oqkv_ref[...] = tn(s.n1[...], s.gqkv[...])
+        for t in range(nh):
+
+            @pl.when(core != t % 2)
+            def _():
+                ra_a[t].wait_send()
+
+        ra_b.wait_send()
         for c in sends:
             c.wait_send()
 
@@ -859,7 +935,16 @@
         ns=((8, D), F32),
     )
     pair = dict(out=((3, R, D), BF16), got=((3, R, D), BF16), mine=((R, D), F32))
-    plan.group(ra=pair, rb=pair, rc=pair)
+    plan.group(rb=pair, rc=pair)
+    plan.group(
+        ra=dict(
+            part=((nh, R, D), F32),
+            out=((nh, R, D), BF16),
+            got=((nh, R, D), BF16),
+            bout=((R, D), BF16),
+            bgot=((R, D), BF16),
+        )
+    )
     if inner:
 
         def weight(width):
@@ -893,10 +978,17 @@
                 yr=((piece, width), BF16),
             )
 
-        wide = weight(FL // 2)
-        plan.group(d0=weight_first(FL // 2), d1=wide, u0=wide, u1=wide)
-        narrow = weight_direct(E)
-        plan.group(o0=narrow, x0=narrow, x1=narrow, x2=narrow)
+        wide, narrow = FL // 2, E
+        plan.group(
+            d0=weight(wide),
+            d1=weight_first(wide),
+            u0=weight(wide),
+            u1=weight_first(wide),
+            o0=weight(narrow),
+            x0=weight(narrow),
+            x1=weight_direct(narrow),
+            x2=weight(narrow),
+        )
         turned = ((D, T), BF16)
         plan.add(n1t=turned, n2t=turned, ogt=turned, gbt=turned)
         plan.add(

time: 99.1 us -> 90.3 us (0.911)
  Pallas kernels: 98.1 us -> 89.3 us
    pallas_call x1, Pallas kernels: 95.6 us -> 86.8 us  [per_device(): build(dims)]
where the time goes in v3:
time: 90.3 us; the launch traced here: 90.1 us
  Pallas kernels  89.3 us (99%)
    pallas_call x1, Pallas kernels, per_device(): build(dims)  86.8 us
    pallas_call x1, Pallas kernels, hand_over(): pl.pallas_call(kernel, out_shape=[jax.ShapeDtypeStruct(a.shape, a.dtype)...  2.54 us

profile of v3, /device:TPU:0, one launch (start us, length us, event | category | flops | bytes accessed | tf_op | source)
XLA Modules:
  0.0 90.1 jit_solution(2370023742486040566)
XLA Ops:
  0.6 86.8 %block.1 = (bf16[1,128,768]{2,1,0:T(8,128)(2,1)}, f32[1,128,768]{2,1,0:T(8,128)}, f32[8,128]{1,0:T(8,128)}, f32[3,96,192]{2,1,0:T(8,128)}, f32[192,96]{1,0:T(8,1...) custom-call(bf16[1,128,768]{2,1,0:T(8,128)(2,1)} %refs_0_.1, s32[1,1024]{1,0:T(1,128)} %refs_1_.1, s32[3,16]{1,0:T(4,128)} %refs_2_.1, ...), custom_call_target="tpu_custom_call" | custom-call | tf_op jit(solution)/shard_map/block/pallas_call | solution.py:1075
  87.4 2.5 %hand_over.1 = (bf16[1,128,768]{2,1,0:T(8,128)(2,1)}, f32[1,128,768]{2,1,0:T(8,128)}, f32[3,96,192]{2,1,0:T(8,128)}, f32[192,96]{1,0:T(8,128)}, f32[96,768]{1,0:...) custom-call(bf16[1,128,768]{2,1,0:T(8,128)(2,1)} %get-tuple-element.27.refs_0_, ...), custom_call_target="tpu_custom_call" | custom-call | tf_op jit(solution)/shard_map/hand_over/pallas_call | solution.py:1040

commit v4 on v3

--- a/solution.py
+++ b/solution.py
@@ -91,13 +91,15 @@
 
     def kernel(*refs):
         (
-            tok_hbm, seg_ref, pat_ref, omega_ref, g1_ref, b1_ref, wqkv_hbm, wout_hbm,
-            g2_ref, b2_ref, wup_hbm, wdown_hbm, og_hbm,
+            tok_hbm, seg_hbm, pat_hbm, omega_hbm, g1_hbm, b1_hbm, wqkv_hbm, wout_hbm,
+            g2_hbm, b2_hbm, wup_hbm, wdown_hbm, og_hbm,
         ) = refs[:n_in]
         (
             mixed_ref, gtok_ref, norm_ref, oqkv_ref, oout_ref, oup_ref, odown_ref,
         ) = refs[n_in : n_in + n_out]
         s = plan.bind(refs[n_in + n_out :])
+        seg_ref, pat_ref, omega_ref = s.seg, s.pat, s.omega
+        g1_ref, b1_ref, g2_ref, b2_ref = s.g1, s.b1, s.g2, s.b2
         ssem, rsem, lsem = s.ssem, s.rsem, s.lsem
         used = {"r": 0, "l": 0}
         sends = []
@@ -116,6 +118,11 @@
             c = pltpu.make_async_copy(src, dst, lsem.at[k])
             c.start()
             return c
+
+        written = []
+
+        def write(src, dst):
+            written.append(local(src, dst))
 
         def send(src, dst, **dev):
             k = used["r"]
@@ -139,18 +146,28 @@
         def rows(slot, n=TILE):
             return pl.ds(pl.multiple_of(slot * n, n), n)
 
-        c_tok = local(tok_hbm.at[0], s.tok.at[head])
-        c_wqkv = local(wqkv_hbm, s.wqkv)
-        c_wout = local(wout_hbm, s.wo.at[head])
-        c_og = local(og_hbm.at[0], s.og.at[head])
-        c_wup = local(wup_hbm, s.wup)
-        c_wdown = local(wdown_hbm, s.wdown)
+        b1 = bat + 1 - 2 * lax.rem(bat, 2)
         barrier = pltpu.get_barrier_semaphore()
         peers = [dict(head=h1), dict(head=h2), dict(head=h3), dict(seq=other)]
         if inner:
             peers += [dict(batch=lax.rem(bat + d, nb)) for d in range(1, nb)]
+        else:
+            peers += [dict(batch=b1)]
         for dev in peers:
             pl.semaphore_signal(barrier, inc=1, device_id=dev, device_id_type=MESH)
+        c_tok = local(tok_hbm.at[0], s.tok.at[head])
+        c_wout = local(wout_hbm, s.wo.at[head])
+        c_og = local(og_hbm.at[0], s.og.at[head])
+        c_wqkv = local(wqkv_hbm, s.wqkv)
+        small = [
+            local(a, b)
+            for a, b in (
+                (seg_hbm, seg_ref), (pat_hbm, pat_ref), (omega_hbm, omega_ref),
+                (g1_hbm, g1_ref), (b1_hbm, b1_ref), (g2_hbm, g2_ref), (b2_hbm, b2_ref),
+            )
+        ]
+        c_wup = local(wup_hbm, s.wup)
+        c_wdown = local(wdown_hbm, s.wdown)
         pl.semaphore_wait(barrier, len(peers))
 
         def gather_start(buf, chunks):
@@ -173,7 +190,17 @@
 
         c_tok.wait()
         ag_tok = gather_start(s.tok, 2)
-
+        c_wout.wait()
+        cut = E // 2
+        half_wo = pl.ds(pl.multiple_of(lax.rem(bat, 2) * cut, cut), cut)
+        part = s.wo.at[head, half_wo]
+        wo_across = send(part, part, head=h2)
+        wo_beside = send(s.wo.at[head], s.wo.at[head], head=h1)
+        c_og.wait()
+        ag_og = gather_start(s.og, 1)
+
+        for c in small:
+            c.wait()
         lane = lax.broadcasted_iota(jnp.int32, (1, LANES), 1)
         low = lane < DH
         ones_lanes = ((lane == DH) | (lane == DH + 1)).astype(F32)
@@ -245,7 +272,6 @@
                 base = (c * H + h) * LANES
                 s.wpad[base : base + DH, :] = src
                 s.wpad[base + DH : base + 2 * DH, :] = src if c < 2 else jnp.zeros_like(src)
-        c_wout.wait()
         for h in range(H):
             s.wopad[h * LANES : h * LANES + DH, :] = s.wo[head, h * DH : (h + 1) * DH, :]
             s.wopad[h * LANES + DH : (h + 1) * LANES, :] = jnp.zeros((DH, D), BF16)
@@ -283,25 +309,26 @@
             beside.wait_recv()
         project(h1)
         fw_tok = gather_forward(s.tok, ag_tok)
-        ag_wo = gather_start(s.wo, 1)
         project(h2)
         for c in fw_tok:
             c.wait_recv()
         project(h3)
 
         for h in range(H):
-            fk = s.fk[h]
-            v = s.v[h].astype(F32)
-            v0 = (v * s.m0[...]).astype(BF16)
-            s.v0[h] = v0
-            s.rout[h] = tn(v0, fk)[:STATE].astype(BF16)
             kk = s.k[h, T - BLK : T, :].astype(F32)
-            vv = v[T - BLK : T, :]
+            vv = s.v[h, T - BLK : T, :].astype(F32)
             s.kvout[h] = jnp.where(low, kk, pltpu.roll(vv, DH, 1)).astype(BF16)
         ex_kv = send(s.kvout, s.kvin, seq=other)
-        ex_r = send(s.rout, s.rin.at[:, pl.ds(0, STATE)], seq=other)
-        c_og.wait()
-        ag_og = gather_start(s.og, 1)
+        ex_r = []
+        for h in range(H):
+            v0 = (s.v[h].astype(F32) * s.m0[...]).astype(BF16)
+            s.v0[h] = v0
+            s.rout[h] = tn(v0, s.fk[h])[:STATE].astype(BF16)
+            ex_r.append(send(s.rout.at[h], s.rin.at[h, pl.ds(0, STATE)], seq=other))
+
+        wo_across.wait_recv()
+        part = s.wo.at[h2, half_wo]
+        wo_batch = send(part, part, batch=b1)
 
         def attend(h, carry):
             for t in range(nt_tiles):
@@ -326,7 +353,6 @@
             return carry
 
         lax.fori_loop(0, H, attend, 0)
-        fw_wo = gather_forward(s.wo, ag_wo)
 
         if inner:
             for j in range(nh):
@@ -334,7 +360,6 @@
                 s.n1t[:, lo : lo + TILE] = jnp.transpose(s.n1[lo : lo + TILE, :])
 
         ex_kv.wait_recv()
-        ex_r.wait_recv()
 
         def unpack(packed):
             x = packed.astype(F32)
@@ -357,13 +382,14 @@
             use_exact = s.thr[h, 0:BLK, 0:BLK] < 2.5
             w_in = jnp.where(same_in, jnp.where(use_exact, exact, low_rank), 0.0).astype(BF16)
             s.win[h] = w_in
+            s.acc[h, 0:BLK, :] = s.acc[h, 0:BLK, :] + nn(w_in, v_in)
+            s.last[h] = tn((v_in.astype(F32) * s.mprev[...]).astype(BF16), f_in)
+        for h in range(H):
+            ex_r[h].wait_recv()
             state = s.rin[h]
-            later = state.astype(F32) * s.link[0:1, :] + tn(
-                (v_in.astype(F32) * s.mprev[...]).astype(BF16), f_in
-            )
-            s.rlater[h] = later.astype(BF16)
-            far0 = jnp.where(s.mfar[0:BLK, :] > 0.5, nt(fq0, state), 0.0)
-            s.acc[h, 0:BLK, :] = s.acc[h, 0:BLK, :] + nn(w_in, v_in) + far0
+            s.rlater[h] = (state.astype(F32) * s.link[0:1, :] + s.last[h]).astype(BF16)
+            far0 = jnp.where(s.mfar[0:BLK, :] > 0.5, nt(s.fq[h, 0:BLK, :], state), 0.0)
+            s.acc[h, 0:BLK, :] = s.acc[h, 0:BLK, :] + far0
             far1 = jnp.where(
                 s.mfar[BLK:T, :] > 0.5, nt(s.fq[h, BLK:T, :], s.rlater[h]), 0.0
             )
@@ -387,11 +413,11 @@
                     s.at[head, lo:hi, h * DH : (h + 1) * DH] = outs[h][:, :DH].astype(BF16)
             part = s.at.at[head, pl.ds(lo, TILE)]
             ag_at[t] = (send(part, part, head=h2), send(part, part, head=h1))
-        for c in fw_wo:
-            c.wait_recv()
-        for _, c, _, _ in ag_wo:
-            c.wait_recv()
+        wo_batch.wait_recv()
+        fw_wo = send(s.wo.at[h2], s.wo.at[h2], head=h1)
         fw_og = gather_forward(s.og, ag_og)
+        wo_beside.wait_recv()
+        fw_wo.wait_recv()
         for _, c, _, _ in ag_og:
             c.wait_recv()
         for c in fw_og:
@@ -443,6 +469,11 @@
             s.n2[at, :] = normed
             act, slope = gelu_both(nn(normed, s.wup[...]))
             s.act[at, :] = act.astype(BF16)
+            s.slope[at, :] = slope
+
+        def feed_back(slot):
+            at = slice(slot * TILE, (slot + 1) * TILE)
+            slope = s.slope[at, :]
             gu = (nt(s.og[slot], s.wdown[...]) * slope).astype(BF16)
             s.gu[at, :] = gu
             s.ra.part[slot] = nt(gu, s.wup[...])
@@ -471,12 +502,7 @@
             if i + 1 < nh:
                 forward_attended(order[i + 1])
             feed(t)
-            to_core(t)
-            if i > 0:
-                to_chip(order[i - 1])
-        to_chip(order[-1])
-
-        b1 = bat + 1 - 2 * lax.rem(bat, 2)
+
         b2 = lax.rem(bat + 2, nb)
         b3 = lax.rem(b1 + 2, nb)
         there = pl.ds(pl.multiple_of(other * half_rows, LANES), half_rows)
@@ -571,24 +597,25 @@
             chunks((s.o0,), s.gbt, s.at.at[head])
             chunks(qkvs, s.n1t, s.gqkv)
             steps = {
-                0: [(first_za, s.d1)],
-                1: [(y_send, s.d0)],
-                5: [(y_send, s.u0)],
-                6: [(first_za, s.u1)],
-                7: [(first_zb, s.d1)],
-                9: [(za_send, s.d0)],
+                0: [(first_za, s.d0), (y_send, s.d1)],
+                5: [(first_za, s.u1), (y_send, s.u0)],
+                8: [(first_zb, s.d0)],
+                9: [(za_send, s.d1)],
                 15: [(first_zb, s.u1)],
                 17: [(y_send, s.o0)],
-                19: [(za_send, s.u0)],
-                21: [(y_send, s.x0)],
-                24: [(zb_send, s.d0)],
-                27: [(za_send, s.o0), (y_send, s.x1)],
-                28: [(zb_send, s.u0), (za_send, s.x0)],
-                29: [(y_send, s.x2), (zb_send, s.o0), (zd_send, s.x1)],
-                30: [(first_y, s.d1)],
-                31: [(za_send, s.x2)],
-                34: [(zb_send, s.x0)],
-                36: [(first_y, s.u1)],
+                18: [(za_send, s.u0)],
+                19: [(y_send, s.x1)],
+                20: [(y_send, s.x0)],
+                22: [(za_send, s.o0)],
+                24: [(zb_send, s.d1)],
+                25: [(y_send, s.x2)],
+                27: [(za_send, s.x1)],
+                28: [(zb_send, s.u0)],
+                31: [(za_send, s.x0), (zb_send, s.x1)],
+                32: [(zb_send, s.o0)],
+                33: [(za_send, s.x2), (first_y, s.u1)],
+                34: [(first_y, s.d0)],
+                35: [(zb_send, s.x0)],
                 37: [(zb_send, s.x2)],
             }
 
@@ -597,7 +624,14 @@
                 for step, group in steps.get(number, ()):
                     step(group)
 
-        run(0, 1)
+        run(0)
+        for i, t in enumerate(order):
+            feed_back(t)
+            to_core(t)
+            if i > 0:
+                to_chip(order[i - 1])
+        to_chip(order[-1])
+        run(1)
         for t in range(nh):
 
             @pl.when(head == t)
@@ -747,6 +781,14 @@
                 s.gbt[:, lo : lo + TILE] = jnp.transpose(s.gb[j])
         run(17)
 
+        if inner:
+            width = D // (ns * nb * nh)
+            start = ((seq * nb + bat) * nh + head) * width
+            s.pick[...] = (
+                lax.broadcasted_iota(jnp.int32, (D, LANES), 0)
+                == lax.broadcasted_iota(jnp.int32, (D, LANES), 1) + start
+            ).astype(F32)
+
         ex_gkv.wait_recv()
         ex_gr.wait_recv()
         run(18)
@@ -776,15 +818,15 @@
             else:
                 s.gqkv[:, i * DH : (i + 1) * DH] = a[:, :DH].astype(BF16)
 
-        run(19, 20, 21, 22)
+        run(19)
 
         def first_grad(slot):
             return nn(s.gqkv[rows(slot), :], s.wqkv[...])
 
         rb_a = scatter_beside(first_grad, s.rb)
-        run(23)
+        run(20)
         rb_b = scatter_across(s.rb, rb_a)
-        run(24)
+        run(21, 22, 23, 24)
         rb_c = scatter_last(first_grad, s.rb)
         run(25)
         own = first_grad(head)
@@ -797,7 +839,7 @@
         xhat1, rstd1 = normalize(s.tok[head].astype(F32))
         s.ns[0:1, :] = jnp.sum(grad1 * xhat1, axis=0, keepdims=True)
         s.ns[1:2, :] = jnp.sum(grad1, axis=0, keepdims=True)
-        gtok_ref[0] = s.gh[...] + norm_back(grad1, gain1, xhat1, rstd1)
+        s.gh[...] = s.gh[...] + norm_back(grad1, gain1, xhat1, rstd1)
 
         if inner:
             run(30)
@@ -811,7 +853,9 @@
             run(32)
             n_y = send(s.ns2, s.ny, seq=other)
             run(33)
-        mixed_ref[0] = (own_mixed + scatter_done(s.rc, rc_b, rc_c)).astype(BF16)
+        write(s.gh, gtok_ref.at[0])
+        s.omixed[...] = (own_mixed + scatter_done(s.rc, rc_b, rc_c)).astype(BF16)
+        write(s.omixed, mixed_ref.at[0])
         if inner:
             run(34)
             n_y.wait_recv()
@@ -822,38 +866,42 @@
             ]
             run(36, 37)
             wide = FL // 2
-            for i in range(2):
-                odown_ref[:, i * wide : (i + 1) * wide] = collect(downs[i])
-                oup_ref[:, i * wide : (i + 1) * wide] = collect(ups[i])
+            for out, groups, ref in ((s.odown, downs, odown_ref), (s.oup, ups, oup_ref)):
+                for i, g in enumerate(groups):
+                    out[:, i * wide : (i + 1) * wide] = collect(g)
+                write(out, ref)
             s.otmp[...] = jnp.zeros_like(s.otmp)
             s.otmp[0:piece, 0:E] = collect(s.o0)
-            oout_ref[...] = jnp.transpose(s.otmp[...])[:E, :piece]
+            s.oout[...] = jnp.transpose(s.otmp[...])[:E, :piece]
+            write(s.oout, oout_ref)
             total = s.ns3[...]
             for i, c in enumerate(n_z):
                 c.wait_recv()
                 total = total + s.nz[i]
-            width = D // (ns * nb * nh)
-            start = ((seq * nb + bat) * nh + head) * width
-            pick = (
-                lax.broadcasted_iota(jnp.int32, (D, LANES), 0)
-                == lax.broadcasted_iota(jnp.int32, (D, LANES), 1) + start
-            ).astype(F32)
-            norm_ref[...] = lax.dot_general(
-                total, pick, (((1,), (0,)), ((), ())),
+            s.onorm[...] = lax.dot_general(
+                total, s.pick[...], (((1,), (0,)), ((), ())),
                 precision=lax.Precision.HIGHEST, preferred_element_type=F32,
             )
+            write(s.onorm, norm_ref)
             for i, g in enumerate(qkvs):
-                oqkv_ref[i] = collect(g)
+                s.oqkv[i] = collect(g)
+                write(s.oqkv.at[i], oqkv_ref.at[i])
         else:
 
             def joined(ref):
                 return jnp.concatenate([ref[j] for j in range(nh)], axis=0)
 
-            norm_ref[...] = s.ns[...]
-            odown_ref[...] = tn(joined(s.og), s.act[...])
-            oup_ref[...] = tn(s.n2[...], s.gu[...])
-            oout_ref[...] = tn(joined(s.gb), s.at[head])
-            oqkv_ref[...] = tn(s.n1[...], s.gqkv[...])
+            write(s.ns, norm_ref)
+            s.odown[...] = tn(joined(s.og), s.act[...])
+            write(s.odown, odown_ref)
+            s.oup[...] = tn(s.n2[...], s.gu[...])
+            write(s.oup, oup_ref)
+            s.oout[...] = tn(joined(s.gb), s.at[head])
+            write(s.oout, oout_ref)
+            s.oqkv[...] = tn(s.n1[...], s.gqkv[...])
+            write(s.oqkv, oqkv_ref)
+        for c in written:
+            c.wait()
         for t in range(nh):
 
             @pl.when(core != t % 2)
@@ -872,7 +920,15 @@
     plan = Plan()
     piece = D // (ns * nb)
     half = D // ns
+    blocks = ns * T // BLK
     plan.add(
+        seg=((1, ns * T), jnp.int32),
+        pat=((H, blocks), jnp.int32),
+        omega=((DH, M), F32),
+        g1=((D,), F32),
+        b1=((D,), F32),
+        g2=((D,), F32),
+        b2=((D,), F32),
         tok=((nh, R, D), BF16),
         og=((nh, R, D), BF16),
         wqkv=((3 * E, D), BF16),
@@ -906,6 +962,7 @@
         rin=((H, LANES, M), BF16),
         grin=((H, LANES, M), BF16),
         rlater=((H, LANES, M), BF16),
+        last=((H, LANES, M), F32),
         kvout=((H, BLK, LANES), BF16),
         kvin=((H, BLK, LANES), BF16),
         gkvout=((H, BLK, LANES), BF16),
@@ -920,6 +977,7 @@
         acc=((H, T, LANES), F32),
         at=((nh, T, E), BF16),
         hid=((T, D), F32),
+        slope=((T, FL), F32),
         n2=((T, D), BF16),
         act=((T, FL), BF16),
         gu=((T, FL), BF16),
@@ -980,16 +1038,24 @@
 
         wide, narrow = FL // 2, E
         plan.group(
-            d0=weight(wide),
-            d1=weight_first(wide),
+            d0=weight_first(wide),
+            d1=weight(wide),
             u0=weight(wide),
             u1=weight_first(wide),
             o0=weight(narrow),
             x0=weight(narrow),
-            x1=weight_direct(narrow),
+            x1=weight(narrow),
             x2=weight(narrow),
         )
         turned = ((D, T), BF16)
+        plan.add(
+            odown=((piece, FL), F32),
+            oup=((piece, FL), F32),
+            oout=((E, piece), F32),
+            oqkv=((3, piece, E), F32),
+            onorm=((8, LANES), F32),
+            pick=((D, LANES), F32),
+        )
         plan.add(n1t=turned, n2t=turned, ogt=turned, gbt=turned)
         plan.add(
             ns2=((8, D), F32),
@@ -999,7 +1065,12 @@
             nh=((3, 8, D), F32),
             otmp=((LANES, 2 * LANES), F32),
         )
-    plan.semaphores(ssem=96, rsem=96, lsem=8)
+    else:
+        plan.add(
+            odown=((D, FL), F32), oup=((D, FL), F32), oout=((D, E), F32), oqkv=((D, 3 * E), F32)
+        )
+    plan.add(omixed=((R, D), BF16))
+    plan.semaphores(ssem=96, rsem=96, lsem=32)
 
     if inner:
         grads = [(3, piece, E), (E, piece), (piece, FL), (piece, FL)]
@@ -1009,17 +1080,17 @@
         norm = (8, D)
     outs = [((1, R, D), BF16), ((1, R, D), F32), (norm, F32)] + [(g, F32) for g in grads]
     hbm = pl.BlockSpec(memory_space=pltpu.HBM)
-    vmem = pl.BlockSpec(memory_space=pltpu.VMEM)
-    in_specs = [hbm, vmem, vmem, vmem, vmem, vmem, hbm, hbm, vmem, vmem, hbm, hbm, hbm]
+    in_specs = [hbm] * 13
+    kind, space = (pltpu.VMEM, pltpu.VMEM) if inner else (jax.ShapeDtypeStruct, pltpu.HBM)
     kernel = make_kernel(dims, len(in_specs), len(outs), plan)
     return pl.pallas_call(
         kernel,
-        out_shape=[jax.ShapeDtypeStruct(shape, dtype) for shape, dtype in outs],
+        out_shape=[kind(shape, dtype) for shape, dtype in outs],
         in_specs=in_specs,
-        out_specs=[vmem] * len(outs),
+        out_specs=[pl.BlockSpec(memory_space=space)] * len(outs),
         scratch_shapes=plan.shapes,
         compiler_params=pltpu.CompilerParams(
-            collective_id=0, has_side_effects=True, vmem_limit_bytes=60 << 20
+            collective_id=0, has_side_effects=True, vmem_limit_bytes=(54 if inner else 60) << 20
         ),
         name="block",
     )
@@ -1043,6 +1114,7 @@
         + [jax.ShapeDtypeStruct((width,), F32)] * 4,
         in_specs=[vmem] * len(arrays),
         out_specs=[vmem] * (count + 4),
+        compiler_params=pltpu.CompilerParams(vmem_limit_bytes=6 << 20),
         name="hand_over",
     )(*arrays)
 
@@ -1072,10 +1144,12 @@
     inner = piece % 16 == 0 and nb == 4
     dims = (nh, ns, nb, T, rows, D, E, FL, E // DH, omega.shape[1], inner)
     w_flat = jnp.transpose(w_qkv, (1, 2, 0)).reshape(3 * E, D)
-    mixed, grad_tokens, norms, g_qkv, g_out, g_up, g_down = build(dims)(
+    arrays = (
         tokens, seg_ids, pattern, omega, norm1_gain, norm1_bias, w_flat, w_out,
         norm2_gain, norm2_bias, w_up, w_down, out_grad,
     )
+    arrays = [pltpu.with_memory_space_constraint(a, pltpu.HBM) for a in arrays]
+    mixed, grad_tokens, norms, g_qkv, g_out, g_up, g_down = build(dims)(*arrays)
     if inner:
         width = D // (ns * nb * nh)
         mixed, grad_tokens, g_qkv, g_out, g_up, g_down, *norms = hand_over(

time: 90.3 us -> 85.3 us (0.945)
  Pallas kernels: 89.3 us -> 84.5 us
    pallas_call x1, Pallas kernels: 86.8 us -> 83.3 us  [per_device(): mixed, grad_tokens, norms, g_qkv, g_out, g_up, g_down = build(dims)(*arrays)]
    pallas_call x1, Pallas kernels: 2.54 us -> 1.25 us  [hand_over(): pl.pallas_call(kernel, out_shape=[jax.ShapeDtypeStruct(a.shape, a.dtype)...]
where the time goes in v4:
time: 85.3 us; the launch traced here: 85.2 us
  Pallas kernels  84.5 us (99%)
    pallas_call x1, Pallas kernels, per_device(): mixed, grad_tokens, norms, g_qkv, g_out, g_up, g_down = build(dims)(*arrays)  83.3 us

profile of v4, /device:TPU:0, one launch (start us, length us, event | category | flops | bytes accessed | tf_op | source)
XLA Modules:
  0.0 85.2 jit_solution(13714446957466600089)
XLA Ops:
  0.6 83.3 %block.1 = (bf16[1,128,768]{2,1,0:T(8,128)(2,1)S(1)}, f32[1,128,768]{2,1,0:T(8,128)S(1)}, f32[8,128]{1,0:T(8,128)S(1)}, f32[3,96,192]{2,1,0:T(8,128)S(1)}, f32[1...) custom-call(bf16[1,128,768]{2,1,0:T(8,128)(2,1)} %refs_0_.1, s32[1,1024]{1,0:T(1,128)} %refs_1_.1, ...), custom_call_target="tpu_custom_call" | custom-call | tf_op jit(solution)/shard_map/block/pallas_call | solution.py:1152
  83.9 1.2 %hand_over.1 = (bf16[1,128,768]{2,1,0:T(8,128)(2,1)}, f32[1,128,768]{2,1,0:T(8,128)}, f32[3,96,192]{2,1,0:T(8,128)}, f32[192,96]{1,0:T(8,128)}, f32[96,768]{1,0:...) custom-call(bf16[1,128,768]{2,1,0:T(8,128)(2,1)S(1)} %get-tuple-element.27.refs_0_, ...), custom_call_target="tpu_custom_call" | custom-call | tf_op jit(solution)/shard_map/hand_over/pallas_call | solution.py:1111

commit v5 on v4

--- a/solution.py
+++ b/solution.py
@@ -122,7 +122,13 @@
         written = []
 
         def write(src, dst):
-            written.append(local(src, dst))
+            if not inner:
+                written.append(local(src, dst))
+
+        s.ogtok = s.gh
+        if inner:
+            s.odown, s.oup, s.oout, s.oqkv = odown_ref, oup_ref, oout_ref, oqkv_ref
+            s.onorm, s.omixed, s.ogtok = norm_ref, mixed_ref.at[0], gtok_ref.at[0]
 
         def send(src, dst, **dev):
             k = used["r"]
@@ -388,12 +394,11 @@
             ex_r[h].wait_recv()
             state = s.rin[h]
             s.rlater[h] = (state.astype(F32) * s.link[0:1, :] + s.last[h]).astype(BF16)
-            far0 = jnp.where(s.mfar[0:BLK, :] > 0.5, nt(s.fq[h, 0:BLK, :], state), 0.0)
-            s.acc[h, 0:BLK, :] = s.acc[h, 0:BLK, :] + far0
-            far1 = jnp.where(
-                s.mfar[BLK:T, :] > 0.5, nt(s.fq[h, BLK:T, :], s.rlater[h]), 0.0
-            )
-            s.acc[h, BLK:T, :] = s.acc[h, BLK:T, :] + far1
+
+        def add_far(h, lo, hi, state):
+            far = nt(s.fq[h, lo:hi, :], state)
+            far = jnp.where(s.mfar[lo:hi, :] > 0.5, far, 0.0)
+            s.acc[h, lo:hi, :] = s.acc[h, lo:hi, :] + far
 
         def divided(h, lo, hi):
             acc = s.acc[h, lo:hi, :]
@@ -404,6 +409,10 @@
         ag_at = {}
         for t in order:
             lo, hi = t * TILE, (t + 1) * TILE
+            for h in range(H):
+                if t == 0:
+                    add_far(h, 0, BLK, s.rin[h])
+                add_far(h, max(lo, BLK), hi, s.rlater[h])
             outs = [divided(h, lo, hi)[0] for h in range(H)]
             for h in range(0, H, 2):
                 if h + 1 < H:
@@ -599,8 +608,8 @@
             steps = {
                 0: [(first_za, s.d0), (y_send, s.d1)],
                 5: [(first_za, s.u1), (y_send, s.u0)],
-                8: [(first_zb, s.d0)],
-                9: [(za_send, s.d1)],
+                9: [(first_zb, s.d0)],
+                10: [(za_send, s.d1)],
                 15: [(first_zb, s.u1)],
                 17: [(y_send, s.o0)],
                 18: [(za_send, s.u0)],
@@ -609,14 +618,12 @@
                 22: [(za_send, s.o0)],
                 24: [(zb_send, s.d1)],
                 25: [(y_send, s.x2)],
-                27: [(za_send, s.x1)],
-                28: [(zb_send, s.u0)],
+                27: [(za_send, s.x1), (zb_send, s.u0)],
                 31: [(za_send, s.x0), (zb_send, s.x1)],
                 32: [(zb_send, s.o0)],
                 33: [(za_send, s.x2), (first_y, s.u1)],
-                34: [(first_y, s.d0)],
-                35: [(zb_send, s.x0)],
-                37: [(zb_send, s.x2)],
+                34: [(first_y, s.d0), (zb_send, s.x0)],
+                36: [(zb_send, s.x2)],
             }
 
         def run(*numbers):
@@ -839,7 +846,7 @@
         xhat1, rstd1 = normalize(s.tok[head].astype(F32))
         s.ns[0:1, :] = jnp.sum(grad1 * xhat1, axis=0, keepdims=True)
         s.ns[1:2, :] = jnp.sum(grad1, axis=0, keepdims=True)
-        s.gh[...] = s.gh[...] + norm_back(grad1, gain1, xhat1, rstd1)
+        s.ogtok[...] = s.gh[...] + norm_back(grad1, gain1, xhat1, rstd1)
 
         if inner:
             run(30)
@@ -1049,11 +1056,6 @@
         )
         turned = ((D, T), BF16)
         plan.add(
-            odown=((piece, FL), F32),
-            oup=((piece, FL), F32),
-            oout=((E, piece), F32),
-            oqkv=((3, piece, E), F32),
-            onorm=((8, LANES), F32),
             pick=((D, LANES), F32),
         )
         plan.add(n1t=turned, n2t=turned, ogt=turned, gbt=turned)
@@ -1067,9 +1069,12 @@
         )
     else:
         plan.add(
-            odown=((D, FL), F32), oup=((D, FL), F32), oout=((D, E), F32), oqkv=((D, 3 * E), F32)
+            odown=((D, FL), F32),
+            oup=((D, FL), F32),
+            oout=((D, E), F32),
+            oqkv=((D, 3 * E), F32),
+            omixed=((R, D), BF16),
         )
-    plan.add(omixed=((R, D), BF16))
     plan.semaphores(ssem=96, rsem=96, lsem=32)
 
     if inner:

time: 85.3 us -> 84.7 us (level)
  no operation moved by 1% of the time
where the time goes in v5:
time: 84.7 us; the launch traced here: 84.5 us
  Pallas kernels  83.9 us (99%)
    pallas_call x1, Pallas kernels, per_device(): mixed, grad_tokens, norms, g_qkv, g_out, g_up, g_down = build(dims)(*arrays)  82.6 us

profile of v5, /device:TPU:0, one launch (start us, length us, event | category | flops | bytes accessed | tf_op | source)
XLA Modules:
  0.0 84.5 jit_solution(4813511251657037682)
XLA Ops:
  0.6 82.6 %block.1 = (bf16[1,128,768]{2,1,0:T(8,128)(2,1)S(1)}, f32[1,128,768]{2,1,0:T(8,128)S(1)}, f32[8,128]{1,0:T(8,128)S(1)}, f32[3,96,192]{2,1,0:T(8,128)S(1)}, f32[1...) custom-call(bf16[1,128,768]{2,1,0:T(8,128)(2,1)} %refs_0_.1, s32[1,1024]{1,0:T(1,128)} %refs_1_.1, ...), custom_call_target="tpu_custom_call" | custom-call | tf_op jit(solution)/shard_map/block/pallas_call | solution.py:1157
  83.3 1.2 %hand_over.1 = (bf16[1,128,768]{2,1,0:T(8,128)(2,1)}, f32[1,128,768]{2,1,0:T(8,128)}, f32[3,96,192]{2,1,0:T(8,128)}, f32[192,96]{1,0:T(8,128)}, f32[96,768]{1,0:...) custom-call(bf16[1,128,768]{2,1,0:T(8,128)(2,1)S(1)} %get-tuple-element.27.refs_0_, ...), custom_call_target="tpu_custom_call" | custom-call | tf_op jit(solution)/shard_map/hand_over/pallas_call | solution.py:1116

commit v6 on v5

--- a/solution.py
+++ b/solution.py
@@ -195,7 +195,7 @@
             return out
 
         c_tok.wait()
-        ag_tok = gather_start(s.tok, 2)
+        ag_tok = gather_start(s.tok, 4)
         c_wout.wait()
         cut = E // 2
         half_wo = pl.ds(pl.multiple_of(lax.rem(bat, 2) * cut, cut), cut)
@@ -615,8 +615,8 @@
                 18: [(za_send, s.u0)],
                 19: [(y_send, s.x1)],
                 20: [(y_send, s.x0)],
+                21: [(zb_send, s.d1)],
                 22: [(za_send, s.o0)],
-                24: [(zb_send, s.d1)],
                 25: [(y_send, s.x2)],
                 27: [(za_send, s.x1), (zb_send, s.u0)],
                 31: [(za_send, s.x0), (zb_send, s.x1)],
@@ -657,7 +657,7 @@
         s.gh[...] = grad_hidden
         s.gb[head] = grad_hidden.astype(BF16)
         run(3)
-        ag_gb = gather_start(s.gb, 2)
+        ag_gb = gather_start(s.gb, 4)
         run(4)
         if inner:
             for j in range(nh):

time: 84.7 us -> 84.5 us (level)
  no operation moved by 1% of the time
where the time goes in v6:
time: 84.5 us; the launch traced here: 84.4 us
  Pallas kernels  83.7 us (99%)
    pallas_call x1, Pallas kernels, per_device(): mixed, grad_tokens, norms, g_qkv, g_out, g_up, g_down = build(dims)(*arrays)  82.5 us

profile of v6, /device:TPU:0, one launch (start us, length us, event | category | flops | bytes accessed | tf_op | source)
XLA Modules:
  0.0 84.4 jit_solution(5676733808327301270)
XLA Ops:
  0.6 82.5 %block.1 = (bf16[1,128,768]{2,1,0:T(8,128)(2,1)S(1)}, f32[1,128,768]{2,1,0:T(8,128)S(1)}, f32[8,128]{1,0:T(8,128)S(1)}, f32[3,96,192]{2,1,0:T(8,128)S(1)}, f32[1...) custom-call(bf16[1,128,768]{2,1,0:T(8,128)(2,1)} %refs_0_.1, s32[1,1024]{1,0:T(1,128)} %refs_1_.1, ...), custom_call_target="tpu_custom_call" | custom-call | tf_op jit(solution)/shard_map/block/pallas_call | solution.py:1157
  83.1 1.2 %hand_over.1 = (bf16[1,128,768]{2,1,0:T(8,128)(2,1)}, f32[1,128,768]{2,1,0:T(8,128)}, f32[3,96,192]{2,1,0:T(8,128)}, f32[192,96]{1,0:T(8,128)}, f32[96,768]{1,0:...) custom-call(bf16[1,128,768]{2,1,0:T(8,128)(2,1)S(1)} %get-tuple-element.27.refs_0_, ...), custom_call_target="tpu_custom_call" | custom-call | tf_op jit(solution)/shard_map/hand_over/pallas_call | solution.py:1116
